TPU v7x, 128 devices: a whole 4x4x4 slice. The times are simulated.
128 devices in a mesh: blade: 32 (over z, y, core), span: 4 (over x).
Axes of the slice: x: 4, y: 4, z: 4, core: 2. Of those that a mesh axis runs over, the one named last changes fastest.
Arguments:
- solid_temp: float32 [8, 2048, 512], P(None, 'blade', 'span'), may hold values from 0.5 to 2.5
- base_conductivity: float32 [8, 2048, 512], P(None, 'blade', 'span'), may hold values from 0.3 to 3
- coolant_htc: float32 [2048, 512], P('blade', 'span'), may hold values from 0.3 to 3
- fluid_temp: float32 [262144], P(('blade', 'span')), may hold values from 1 to 3
- wall_htc: float32 [262144], P(('blade', 'span')), may hold values from 0.2 to 5
- face_dest: int32 [262144, 1], P(('blade', 'span')), may hold values from 0 to 127; in each aligned block of 2048 rows (0 to 2047, 2048 to 4095, ...) at most 32 rows name the same one
- face_cell: int32 [262144], P(('blade', 'span')), may hold values from 0 to 8191
- face_count: int32 [128], P(('blade', 'span')), may hold values from 1 to 2048, 196608 in all
Outputs:
- solid_out: float32 [8, 2048, 512], P(None, 'blade', 'span')
- fluid_out: float32 [262144], P(('blade', 'span'))
- wall_flux: float32 [262144], P(('blade', 'span'))
Inputs may be any that keep to these rules, and one draw needn't show every extreme that they name: `face_dest`: among the 2048 slots of any one device no solid device is named by more than 32 slots, and some device's slots name one solid device exactly 32 times. `face_count`: some device has all 2048 slots live.
All inputs are finite; a program needn't handle non-finite values.
Results may differ from a plain program's by a relative error of at most 0.0003.
Values sent between devices are 32-bit elements; how exact they have to be, the bound alone decides.
A program may use at most 64 MiB of HBM per device.

v0:
```python
import jax
import jax.numpy as jnp
from jax import lax
from jax.sharding import PartitionSpec as P

SWEEPS = 6
SUBITERS = 4


def extended(cells, sides, width):
    for axis, dim in sides:
        count = lax.axis_size(axis)
        ends = count - 1
        head = lax.slice_in_dim(cells, 0, width, axis=dim)
        tail = lax.slice_in_dim(cells, cells.shape[dim] - width, cells.shape[dim], axis=dim)
        cells = jnp.concatenate(
            [
                lax.ppermute(tail, axis, [(i, (i + 1) % count) for i in range(ends)]),
                cells,
                lax.ppermute(head, axis, [((i + 1) % count, i) for i in range(ends)]),
            ],
            axis=dim,
        )
    return cells


def shifted(arr, a, b, c):
    n0, n1, n2 = arr.shape
    return arr[1 + a : n0 - 1 + a, 1 + b : n1 - 1 + b, 1 + c : n2 - 1 + c]


def relax(padded_temp, padded_kappa, heat, heat_temp, coolant):
    cond = padded_kappa * (1.0 + 0.25 * padded_temp * padded_temp)
    centre = shifted(cond, 0, 0, 0)
    numer = jnp.zeros(centre.shape, jnp.float32)
    denom = jnp.zeros(centre.shape, jnp.float32)
    for a, b, c in ((1, 0, 0), (-1, 0, 0), (0, 1, 0), (0, -1, 0), (0, 0, 1), (0, 0, -1)):
        other = shifted(cond, a, b, c)
        weight = 2.0 * centre * other / (centre + other)
        numer = numer + weight * shifted(padded_temp, a, b, c)
        denom = denom + weight
    numer = numer.at[0].add(heat_temp)
    denom = denom.at[0].add(heat)
    denom = denom.at[-1].add(coolant)
    return numer / denom


def layer_pad(field):
    return jnp.pad(field, ((1, 1), (0, 0), (0, 0)))


def sweep(temp, kappa_pad, heat, heat_temp, coolant):
    padded = extended(temp, (("blade", 1), ("span", 2)), 1)
    return relax(layer_pad(padded), kappa_pad, heat, heat_temp, coolant)


def shards(
    solid_temp,
    base_conductivity,
    coolant_htc,
    fluid_temp,
    wall_htc,
    face_dest,
    face_cell,
    face_count,
):
    n_blade = lax.axis_size("blade")
    n_span = lax.axis_size("span")
    devices = n_blade * n_span
    slots_dev = fluid_temp.shape[0]
    cap = max(slots_dev // 64, 2 * slots_dev // devices)
    layers, cells_x, cells_s = solid_temp.shape
    surface = cells_x * cells_s
    dest = face_dest.reshape(-1)
    live = jnp.arange(slots_dev, dtype=jnp.int32) < face_count[0]
    blocks = slots_dev // 128
    onehot = (
        (
            dest.reshape(blocks, 128)[:, :, None]
            == jnp.arange(devices, dtype=jnp.int32)[None, None, :]
        )
        & live.reshape(blocks, 128)[:, :, None]
    ).astype(jnp.bfloat16)
    lower = (jnp.arange(128)[:, None] > jnp.arange(128)[None, :]).astype(jnp.bfloat16)
    before = jnp.einsum("ij,bjd->bid", lower, onehot, preferred_element_type=jnp.float32)
    counts = jnp.sum(onehot, axis=1, dtype=jnp.float32)
    offsets = jnp.cumsum(counts, axis=0) - counts
    position = jnp.sum((before + offsets[:, None, :]) * onehot, axis=-1, dtype=jnp.float32)
    rank = position.reshape(-1).astype(jnp.int32)
    slot = jnp.where(live, dest * cap + rank, devices * cap)
    safe_slot = jnp.minimum(slot, devices * cap - 1)

    def pack(values):
        filled = jnp.zeros((devices * cap,), values.dtype).at[slot].set(values, mode="drop")
        return filled.reshape(devices, cap)

    htc_recv, cell_recv = (
        lax.all_to_all(pack(wall_htc), ("blade", "span"), split_axis=0, concat_axis=0, tiled=True),
        lax.all_to_all(pack(face_cell), ("blade", "span"), split_axis=0, concat_axis=0, tiled=True),
    )
    htc_recv = htc_recv.reshape(-1)
    cell_recv = cell_recv.reshape(-1)
    heat = jax.ops.segment_sum(htc_recv, cell_recv, num_segments=surface).reshape(cells_x, cells_s)
    kappa_pad = layer_pad(extended(base_conductivity, (("blade", 1), ("span", 2)), 1))
    temp = solid_temp
    tf = fluid_temp
    flux = jnp.zeros_like(fluid_temp)
    for outer in range(SUBITERS):
        tf_recv = lax.all_to_all(
            pack(tf), ("blade", "span"), split_axis=0, concat_axis=0, tiled=True
        )
        tf_recv = tf_recv.reshape(-1)
        heat_temp = jax.ops.segment_sum(
            htc_recv * tf_recv, cell_recv, num_segments=surface
        ).reshape(cells_x, cells_s)
        for inner in range(SWEEPS):
            temp = sweep(temp, kappa_pad, heat, heat_temp, coolant_htc)
        wall_slots = temp[0].reshape(-1)[cell_recv].reshape(devices, cap)
        wall_back = lax.all_to_all(
            wall_slots, ("blade", "span"), split_axis=0, concat_axis=0, tiled=True
        )
        wall_face = jnp.take(wall_back.reshape(-1), safe_slot)
        q = wall_htc * (tf - wall_face)
        tf = jnp.where(live, tf - q / (wall_htc + 2.0), tf)
        flux = jnp.where(live, q, 0.0)
    return (temp, tf, flux)


def solution(mesh):
    placed = (
        P(None, "blade", "span"),
        P(None, "blade", "span"),
        P("blade", "span"),
        P(("blade", "span")),
        P(("blade", "span")),
        P(("blade", "span"), None),
        P(("blade", "span")),
        P(("blade", "span")),
    )
    return jax.shard_map(
        shards,
        mesh=mesh,
        in_specs=placed,
        out_specs=(P(None, "blade", "span"), P(("blade", "span")), P(("blade", "span"))),
        check_vma=False,
    )
```

profile of v0, /device:TPU:1, one launch (start us, length us, event | category | flops | bytes accessed | tf_op | source)
XLA Modules:
  0.0 1005.7 jit_solution(950787673934886223)
XLA Ops:
  27.4 8.2 scatter_custom_fusion
  36.4 13.9 %all-to-all-start = ((s32[128,1,32]{2,1,0:T(1,128)}), s32[128,1,32]{2,1,0:T(1,128)S(1)}, u32[]{:S(2)}, u32[]{:S(2)}) async-start(s32[128,1,32]{2,1,0:T(1,128)} %bitcast.6), calls=%async_computation | async-start | bytes 131072 | tf_op jit(solution)/shard_map/all_to_all | solution.py:99
  50.2 8.2 scatter_custom_fusion.1
  59.2 8.2 scatter_custom_fusion.2
  70.6 9.8 all-to-all-start.1
  81.2 8.8 all-to-all-done.1
  97.6 6.4 all-to-all-done.2
  104.9 23.1 %scatter_custom_fusion.4 = f32[8192]{0:T(1024)S(1)} fusion(s32[4096]{0:T(1024)S(1)} %reshape.2031, f32[4096]{0:T(1024)S(1)} %reshape.2041, f32[]{:T(128)} %constant.1483.clone.1), kind=kCustom, calls=%fused_computation.1013 | custom fusion | flops 4096 | bytes 32772 | tf_op jit(solution)/shard_map/scatter-add | solution.py:103
  128.0 22.9 %scatter_custom_fusion.3 = f32[8192]{0:T(1024)S(1)} fusion(s32[4096]{0:T(1024)S(1)} %reshape.2031, f32[4096]{0:T(1024)S(1)} %mul.1328, f32[]{:T(128)} %constant.1483.clone.1), kind=kCustom, calls=%fused_computation.1015 | custom fusion | flops 4096 | bytes 32772 | tf_op jit(solution)/shard_map/scatter-add | solution.py:113
  151.7 7.1 collective-permute-start.9
  165.3 4.9 collective-permute-done.10
  188.9 5.2 collective-permute-done.14
  211.6 5.3 collective-permute-done.18
  232.3 5.2 collective-permute-done.22
  237.4 4.4 collective-permute-done.23
  253.3 4.7 collective-permute-done.26
  266.2 5.0 collective-permute-start.28
  275.3 23.0 %gather_fusion = f32[4096]{0:T(1024)S(1)} fusion(f32[8192]{0:T(1024)S(1)} %slice_bitcast_fusion.3, s32[4096]{0:T(1024)S(1)} %broadcast_clamp_fusion), kind=kCustom, calls=%fused_computation.4 | custom fusion | bytes 49152 | tf_op jit(solution)/shard_map/gather | solution.py:118
  299.1 14.6 %all-to-all-start.3 = ((f32[128,1,32]{2,1,0:T(1,128)}), f32[128,1,32]{2,1,0:T(1,128)S(1)}, u32[]{:S(2)}, u32[]{:S(2)}) async-start(f32[128,1,32]{2,1,0:T(1,128)} %bitcast.16), calls=%async_computation.3 | async-start | bytes 131072 | tf_op jit(solution)/shard_map/all_to_all | solution.py:119
  315.4 7.9 all-to-all-done.3
  324.2 11.8 %gather_fusion.4 = f32[2048]{0:T(1024)S(1)} fusion(f32[4096]{0:T(1024)S(1)} %reshape.1931, s32[2048]{0:T(1024)S(1)} %broadcast_clamp_fusion.1), kind=kCustom, calls=%fused_computation.clone | custom fusion | bytes 24576 | tf_op jit(solution)/shard_map/jit(_take)/gather | solution.py:122
  336.0 8.2 scatter_custom_fusion.5
  349.2 9.6 all-to-all-done.4
  359.7 22.9 %scatter_custom_fusion.6 = f32[8192]{0:T(1024)S(1)} fusion(s32[4096]{0:T(1024)S(1)} %reshape.2031, f32[4096]{0:T(1024)S(1)} %mul.1427, f32[]{:T(128)} %constant.1483.clone.1), kind=kCustom, calls=%fused_computation.1011 | custom fusion | flops 4096 | bytes 32772 | tf_op jit(solution)/shard_map/scatter-add | solution.py:113
  382.7 4.8 collective-permute-start.33
  394.2 4.9 collective-permute-done.34
  417.2 4.8 collective-permute-done.38
  439.5 5.3 collective-permute-done.42
  460.1 5.2 collective-permute-done.46
  465.3 4.4 collective-permute-done.47
  481.3 4.5 collective-permute-done.50
  493.7 5.4 collective-permute-start.52
  503.2 23.0 %gather_fusion.1 = f32[4096]{0:T(1024)S(1)} fusion(f32[8192]{0:T(1024)S(1)} %slice_bitcast_fusion.2, s32[4096]{0:T(1024)S(1)} %broadcast_clamp_fusion), kind=kCustom, calls=%fused_computation.5 | custom fusion | bytes 49152 | tf_op jit(solution)/shard_map/gather | solution.py:118
  527.0 14.8 %all-to-all-start.5 = ((f32[128,1,32]{2,1,0:T(1,128)}), f32[128,1,32]{2,1,0:T(1,128)S(1)}, u32[]{:S(2)}, u32[]{:S(2)}) async-start(f32[128,1,32]{2,1,0:T(1,128)} %bitcast.20), calls=%async_computation.5 | async-start | bytes 131072 | tf_op jit(solution)/shard_map/all_to_all | solution.py:119
  543.5 7.9 all-to-all-done.5
  552.3 11.8 %gather_fusion.5 = f32[2048]{0:T(1024)S(1)} fusion(f32[4096]{0:T(1024)S(1)} %reshape.1934, s32[2048]{0:T(1024)S(1)} %broadcast_clamp_fusion.1), kind=kCustom, calls=%fused_computation.1.clone | custom fusion | bytes 24576 | tf_op jit(solution)/shard_map/jit(_take)/gather | solution.py:122
  564.1 8.2 scatter_custom_fusion.7
  577.3 9.6 all-to-all-done.6
  587.8 22.9 %scatter_custom_fusion.8 = f32[8192]{0:T(1024)S(1)} fusion(s32[4096]{0:T(1024)S(1)} %reshape.2031, f32[4096]{0:T(1024)S(1)} %mul.1525, f32[]{:T(128)} %constant.1483.clone.1), kind=kCustom, calls=%fused_computation.1009 | custom fusion | flops 4096 | bytes 32772 | tf_op jit(solution)/shard_map/scatter-add | solution.py:113
  610.7 4.8 collective-permute-start.57
  622.2 4.9 collective-permute-done.58
  644.8 5.2 collective-permute-done.62
  667.7 5.1 collective-permute-done.66
  688.2 5.2 collective-permute-done.70
  693.4 4.4 collective-permute-done.71
  709.4 4.5 collective-permute-done.74
  721.8 5.4 collective-permute-start.76
  731.3 23.0 %gather_fusion.2 = f32[4096]{0:T(1024)S(1)} fusion(f32[8192]{0:T(1024)S(1)} %slice_bitcast_fusion.1, s32[4096]{0:T(1024)S(1)} %broadcast_clamp_fusion), kind=kCustom, calls=%fused_computation.6 | custom fusion | bytes 49152 | tf_op jit(solution)/shard_map/gather | solution.py:118
  755.0 14.5 %all-to-all-start.7 = ((f32[128,1,32]{2,1,0:T(1,128)}), f32[128,1,32]{2,1,0:T(1,128)S(1)}, u32[]{:S(2)}, u32[]{:S(2)}) async-start(f32[128,1,32]{2,1,0:T(1,128)} %bitcast.24), calls=%async_computation.7 | async-start | bytes 131072 | tf_op jit(solution)/shard_map/all_to_all | solution.py:119
  771.3 7.9 all-to-all-done.7
  780.1 11.8 %gather_fusion.6 = f32[2048]{0:T(1024)S(1)} fusion(f32[4096]{0:T(1024)S(1)} %reshape.1937, s32[2048]{0:T(1024)S(1)} %broadcast_clamp_fusion.1), kind=kCustom, calls=%fused_computation.2.clone | custom fusion | bytes 24576 | tf_op jit(solution)/shard_map/jit(_take)/gather | solution.py:122
  791.9 8.2 scatter_custom_fusion.9
  800.8 4.8 all-to-all-start.8
  805.6 9.6 all-to-all-done.8
  816.1 22.9 %scatter_custom_fusion.10 = f32[8192]{0:T(1024)S(1)} fusion(s32[4096]{0:T(1024)S(1)} %reshape.2031, f32[4096]{0:T(1024)S(1)} %mul.1623, f32[]{:T(128)} %constant.1483.clone.1), kind=kCustom, calls=%fused_computation.1007 | custom fusion | flops 4096 | bytes 32772 | tf_op jit(solution)/shard_map/scatter-add | solution.py:113
  839.0 4.8 collective-permute-start.81
  850.5 4.9 collective-permute-done.82
  873.1 5.2 collective-permute-done.86
  895.8 5.3 collective-permute-done.90
  916.5 5.2 collective-permute-done.94
  921.7 4.4 collective-permute-done.95
  948.1 23.0 %gather_fusion.3 = f32[4096]{0:T(1024)S(1)} fusion(f32[8192]{0:T(1024)S(1)} %slice_bitcast_fusion, s32[4096]{0:T(1024)S(1)} %broadcast_clamp_fusion), kind=kCustom, calls=%fused_computation.7 | custom fusion | bytes 49152 | tf_op jit(solution)/shard_map/gather | solution.py:118
  971.2 21.0 %all_to_all.90 = f32[128,1,32]{2,1,0:T(1,128)S(1)} all-to-all(f32[128,1,32]{2,1,0:T(1,128)S(1)} %bitcast.133), channel_id=1, replica_groups=mesh['blade'=32,'span'=4] {'blade','span'}, dimensions={0} | all-to-all | bytes 32768 | tf_op jit(solution)/shard_map/all_to_all | solution.py:119
  993.1 11.8 %gather_fusion.7 = f32[2048]{0:T(1024)S(1)} fusion(f32[4096]{0:T(1024)S(1)} %reshape.1940, s32[2048]{0:T(1024)S(1)} %broadcast_clamp_fusion.1), kind=kCustom, calls=%fused_computation.3.clone | custom fusion | bytes 24576 | tf_op jit(solution)/shard_map/jit(_take)/gather | solution.py:122
  (499 shorter events, 386.7 us)
Async XLA Ops:
  1.4 14.5 %collective-permute-start.1 = (f32[8,1,128]{2,1,0:T(1,128)S(1)}, f32[8,1,128]{2,1,0:T(1,128)S(1)}, u32[]{:S(2)}, u32[]{:S(2)}) collective-permute-start(f32[8,1,128]{2,1,0:T(1,128)S(1)} %get-tuple-element.1016), channel_id=1, source_target_pairs={{4,0},{8,4},{12,8},{16,12},{20,16},{24,20},{28,24},{32,28},{36,32}... | collective-permute-start | bytes 12296 | tf_op jit(solution)/shard_map/ppermute | solution.py:20
  4.7 11.2 %collective-permute-start = (f32[8,1,128]{2,1,0:T(1,128)S(1)}, f32[8,1,128]{2,1,0:T(1,128)S(1)}, u32[]{:S(2)}, u32[]{:S(2)}) collective-permute-start(f32[8,1,128]{2,1,0:T(1,128)S(1)} %get-tuple-element.1015), channel_id=1, source_target_pairs={{0,4},{4,8},{8,12},{12,16},{16,20},{20,24},{24,28},{28,32},{32,36}... | collective-permute-start | bytes 12296 | tf_op jit(solution)/shard_map/ppermute | solution.py:18
  8.7 13.1 %collective-permute-start.5 = (f32[8,1,128]{2,1,0:T(1,128)S(1)}, f32[8,1,128]{2,1,0:T(1,128)S(1)}, u32[]{:S(2)}, u32[]{:S(2)}) collective-permute-start(f32[8,1,128]{2,1,0:T(1,128)S(1)} %get-tuple-element.1018), channel_id=1, source_target_pairs={{4,0},{8,4},{12,8},{16,12},{20,16},{24,20},{28,24},{32,28},{36,32}... | collective-permute-start | bytes 12296 | tf_op jit(solution)/shard_map/ppermute | solution.py:20
  10.7 11.2 %collective-permute-start.4 = (f32[8,1,128]{2,1,0:T(1,128)S(1)}, f32[8,1,128]{2,1,0:T(1,128)S(1)}, u32[]{:S(2)}, u32[]{:S(2)}) collective-permute-start(f32[8,1,128]{2,1,0:T(1,128)S(1)} %get-tuple-element.1017), channel_id=1, source_target_pairs={{0,4},{4,8},{8,12},{12,16},{16,20},{20,24},{24,28},{28,32},{32,36}... | collective-permute-start | bytes 12296 | tf_op jit(solution)/shard_map/ppermute | solution.py:18
  16.5 51.6 %collective-permute-start.3 = (f32[8,66,1]{2,1,0:T(8,128)S(1)}, f32[8,66,1]{2,1,0:T(8,128)S(1)}, u32[]{:S(2)}, u32[]{:S(2)}) collective-permute-start(f32[8,66,1]{2,1,0:T(8,128)S(1)} %get-tuple-element.966), channel_id=1, source_target_pairs={{1,0},{2,1},{3,2},{5,4},{6,5},{7,6},{9,8},{10,9},{11,10},{13,12},{... | collective-permute-start | bytes 6344 | tf_op jit(solution)/shard_map/ppermute | solution.py:20
  17.8 50.3 %collective-permute-start.2 = (f32[8,66,1]{2,1,0:T(8,128)S(1)}, f32[8,66,1]{2,1,0:T(8,128)S(1)}, u32[]{:S(2)}, u32[]{:S(2)}) collective-permute-start(f32[8,66,1]{2,1,0:T(8,128)S(1)} %get-tuple-element.965), channel_id=1, source_target_pairs={{0,1},{1,2},{2,3},{4,5},{5,6},{6,7},{8,9},{9,10},{10,11},{12,13},{... | collective-permute-start | bytes 6344 | tf_op jit(solution)/shard_map/ppermute | solution.py:18
  22.1 46.1 %collective-permute-start.7 = (f32[8,66,1]{2,1,0:T(8,128)S(1)}, f32[8,66,1]{2,1,0:T(8,128)S(1)}, u32[]{:S(2)}, u32[]{:S(2)}) collective-permute-start(f32[8,66,1]{2,1,0:T(8,128)S(1)} %get-tuple-element.967), channel_id=1, source_target_pairs={{1,0},{2,1},{3,2},{5,4},{6,5},{7,6},{9,8},{10,9},{11,10},{13,12},{... | collective-permute-start | bytes 6344 | tf_op jit(solution)/shard_map/ppermute | solution.py:20
  23.4 45.6 %collective-permute-start.6 = (f32[8,66,1]{2,1,0:T(8,128)S(1)}, f32[8,66,1]{2,1,0:T(8,128)S(1)}, u32[]{:S(2)}, u32[]{:S(2)}) collective-permute-start(f32[8,66,1]{2,1,0:T(8,128)S(1)} %get-tuple-element.968), channel_id=1, source_target_pairs={{0,1},{1,2},{2,3},{4,5},{5,6},{6,7},{8,9},{9,10},{10,11},{12,13},{... | collective-permute-start | bytes 6344 | tf_op jit(solution)/shard_map/ppermute | solution.py:18
  36.4 34.2 %all-to-all-start = ((s32[128,1,32]{2,1,0:T(1,128)}), s32[128,1,32]{2,1,0:T(1,128)S(1)}, u32[]{:S(2)}, u32[]{:S(2)}) async-start(s32[128,1,32]{2,1,0:T(1,128)} %bitcast.6), calls=%async_computation | async-start | bytes 131072 | tf_op jit(solution)/shard_map/all_to_all | solution.py:99
  70.6 19.5 %all-to-all-start.1 = ((f32[128,1,32]{2,1,0:T(1,128)}), f32[128,1,32]{2,1,0:T(1,128)S(1)}, u32[]{:S(2)}, u32[]{:S(2)}) async-start(f32[128,1,32]{2,1,0:T(1,128)} %bitcast.7), calls=%async_computation.1 | async-start | bytes 131072 | tf_op jit(solution)/shard_map/all_to_all | solution.py:98
  90.1 14.0 %all-to-all-start.2 = ((f32[128,1,32]{2,1,0:T(1,128)}), f32[128,1,32]{2,1,0:T(1,128)S(1)}, u32[]{:S(2)}, u32[]{:S(2)}) async-start(f32[128,1,32]{2,1,0:T(1,128)} %bitcast.8), calls=%async_computation.2 | async-start | bytes 131072 | tf_op jit(solution)/shard_map/all_to_all | solution.py:109
  151.7 9.3 collective-permute-start.9
  162.0 8.2 collective-permute-start.10
  164.0 10.0 collective-permute-start.11
  183.6 10.5 %collective-permute-start.14 = (f32[8,66,1]{2,1,0:T(8,128)S(1)}, f32[8,66,1]{2,1,0:T(8,128)S(1)}, u32[]{:S(2)}, u32[]{:S(2)}) collective-permute-start(f32[8,66,1]{2,1,0:T(8,128)S(1)} %get-tuple-element.962), channel_id=1, source_target_pairs={{0,1},{1,2},{2,3},{4,5},{5,6},{6,7},{8,9},{9,10},{10,11},{12,13},{... | collective-permute-start | bytes 6344 | tf_op jit(solution)/shard_map/ppermute | solution.py:18
  187.6 10.7 %collective-permute-start.15 = (f32[8,66,1]{2,1,0:T(8,128)S(1)}, f32[8,66,1]{2,1,0:T(8,128)S(1)}, u32[]{:S(2)}, u32[]{:S(2)}) collective-permute-start(f32[8,66,1]{2,1,0:T(8,128)S(1)} %get-tuple-element.961), channel_id=1, source_target_pairs={{1,0},{2,1},{3,2},{5,4},{6,5},{7,6},{9,8},{10,9},{11,10},{13,12},{... | collective-permute-start | bytes 6344 | tf_op jit(solution)/shard_map/ppermute | solution.py:20
  206.6 10.2 %collective-permute-start.18 = (f32[8,66,1]{2,1,0:T(8,128)S(1)}, f32[8,66,1]{2,1,0:T(8,128)S(1)}, u32[]{:S(2)}, u32[]{:S(2)}) collective-permute-start(f32[8,66,1]{2,1,0:T(8,128)S(1)} %get-tuple-element.960), channel_id=1, source_target_pairs={{0,1},{1,2},{2,3},{4,5},{5,6},{6,7},{8,9},{9,10},{10,11},{12,13},{... | collective-permute-start | bytes 6344 | tf_op jit(solution)/shard_map/ppermute | solution.py:18
  210.3 10.9 %collective-permute-start.19 = (f32[8,66,1]{2,1,0:T(8,128)S(1)}, f32[8,66,1]{2,1,0:T(8,128)S(1)}, u32[]{:S(2)}, u32[]{:S(2)}) collective-permute-start(f32[8,66,1]{2,1,0:T(8,128)S(1)} %get-tuple-element.959), channel_id=1, source_target_pairs={{1,0},{2,1},{3,2},{5,4},{6,5},{7,6},{9,8},{10,9},{11,10},{13,12},{... | collective-permute-start | bytes 6344 | tf_op jit(solution)/shard_map/ppermute | solution.py:20
  229.4 8.0 collective-permute-start.22
  231.0 10.9 %collective-permute-start.23 = (f32[8,66,1]{2,1,0:T(8,128)S(1)}, f32[8,66,1]{2,1,0:T(8,128)S(1)}, u32[]{:S(2)}, u32[]{:S(2)}) collective-permute-start(f32[8,66,1]{2,1,0:T(8,128)S(1)} %get-tuple-element.957), channel_id=1, source_target_pairs={{1,0},{2,1},{3,2},{5,4},{6,5},{7,6},{9,8},{10,9},{11,10},{13,12},{... | collective-permute-start | bytes 6344 | tf_op jit(solution)/shard_map/ppermute | solution.py:20
  250.1 7.8 collective-permute-start.26
  251.7 10.3 %collective-permute-start.27 = (f32[8,66,1]{2,1,0:T(8,128)S(1)}, f32[8,66,1]{2,1,0:T(8,128)S(1)}, u32[]{:S(2)}, u32[]{:S(2)}) collective-permute-start(f32[8,66,1]{2,1,0:T(8,128)S(1)} %get-tuple-element.955), channel_id=1, source_target_pairs={{1,0},{2,1},{3,2},{5,4},{6,5},{7,6},{9,8},{10,9},{11,10},{13,12},{... | collective-permute-start | bytes 6344 | tf_op jit(solution)/shard_map/ppermute | solution.py:20
  272.1 41.6 %collective-permute-start.30 = (f32[8,66,1]{2,1,0:T(8,128)S(1)}, f32[8,66,1]{2,1,0:T(8,128)S(1)}, u32[]{:S(2)}, u32[]{:S(2)}) collective-permute-start(f32[8,66,1]{2,1,0:T(8,128)S(1)} %get-tuple-element.954), channel_id=1, source_target_pairs={{0,1},{1,2},{2,3},{4,5},{5,6},{6,7},{8,9},{9,10},{10,11},{12,13},{... | collective-permute-start | bytes 6344 | tf_op jit(solution)/shard_map/ppermute | solution.py:18
  274.0 39.7 %collective-permute-start.31 = (f32[8,66,1]{2,1,0:T(8,128)S(1)}, f32[8,66,1]{2,1,0:T(8,128)S(1)}, u32[]{:S(2)}, u32[]{:S(2)}) collective-permute-start(f32[8,66,1]{2,1,0:T(8,128)S(1)} %get-tuple-element.953), channel_id=1, source_target_pairs={{1,0},{2,1},{3,2},{5,4},{6,5},{7,6},{9,8},{10,9},{11,10},{13,12},{... | collective-permute-start | bytes 6344 | tf_op jit(solution)/shard_map/ppermute | solution.py:20
  299.1 24.2 %all-to-all-start.3 = ((f32[128,1,32]{2,1,0:T(1,128)}), f32[128,1,32]{2,1,0:T(1,128)S(1)}, u32[]{:S(2)}, u32[]{:S(2)}) async-start(f32[128,1,32]{2,1,0:T(1,128)} %bitcast.16), calls=%async_computation.3 | async-start | bytes 131072 | tf_op jit(solution)/shard_map/all_to_all | solution.py:119
  345.0 13.9 %all-to-all-start.4 = ((f32[128,1,32]{2,1,0:T(1,128)}), f32[128,1,32]{2,1,0:T(1,128)S(1)}, u32[]{:S(2)}, u32[]{:S(2)}) async-start(f32[128,1,32]{2,1,0:T(1,128)} %bitcast.17), calls=%async_computation.4 | async-start | bytes 131072 | tf_op jit(solution)/shard_map/all_to_all | solution.py:109
  390.8 8.3 collective-permute-start.34
  392.9 10.0 collective-permute-start.35
  411.7 10.3 %collective-permute-start.38 = (f32[8,66,1]{2,1,0:T(8,128)S(1)}, f32[8,66,1]{2,1,0:T(8,128)S(1)}, u32[]{:S(2)}, u32[]{:S(2)}) collective-permute-start(f32[8,66,1]{2,1,0:T(8,128)S(1)} %get-tuple-element.950), channel_id=1, source_target_pairs={{0,1},{1,2},{2,3},{4,5},{5,6},{6,7},{8,9},{9,10},{10,11},{12,13},{... | collective-permute-start | bytes 6344 | tf_op jit(solution)/shard_map/ppermute | solution.py:18
  415.4 10.7 %collective-permute-start.39 = (f32[8,66,1]{2,1,0:T(8,128)S(1)}, f32[8,66,1]{2,1,0:T(8,128)S(1)}, u32[]{:S(2)}, u32[]{:S(2)}) collective-permute-start(f32[8,66,1]{2,1,0:T(8,128)S(1)} %get-tuple-element.949), channel_id=1, source_target_pairs={{1,0},{2,1},{3,2},{5,4},{6,5},{7,6},{9,8},{10,9},{11,10},{13,12},{... | collective-permute-start | bytes 6344 | tf_op jit(solution)/shard_map/ppermute | solution.py:20
  434.5 10.3 %collective-permute-start.42 = (f32[8,66,1]{2,1,0:T(8,128)S(1)}, f32[8,66,1]{2,1,0:T(8,128)S(1)}, u32[]{:S(2)}, u32[]{:S(2)}) collective-permute-start(f32[8,66,1]{2,1,0:T(8,128)S(1)} %get-tuple-element.948), channel_id=1, source_target_pairs={{0,1},{1,2},{2,3},{4,5},{5,6},{6,7},{8,9},{9,10},{10,11},{12,13},{... | collective-permute-start | bytes 6344 | tf_op jit(solution)/shard_map/ppermute | solution.py:18
  438.2 10.9 %collective-permute-start.43 = (f32[8,66,1]{2,1,0:T(8,128)S(1)}, f32[8,66,1]{2,1,0:T(8,128)S(1)}, u32[]{:S(2)}, u32[]{:S(2)}) collective-permute-start(f32[8,66,1]{2,1,0:T(8,128)S(1)} %get-tuple-element.947), channel_id=1, source_target_pairs={{1,0},{2,1},{3,2},{5,4},{6,5},{7,6},{9,8},{10,9},{11,10},{13,12},{... | collective-permute-start | bytes 6344 | tf_op jit(solution)/shard_map/ppermute | solution.py:20
  457.3 8.0 collective-permute-start.46
  458.8 10.9 %collective-permute-start.47 = (f32[8,66,1]{2,1,0:T(8,128)S(1)}, f32[8,66,1]{2,1,0:T(8,128)S(1)}, u32[]{:S(2)}, u32[]{:S(2)}) collective-permute-start(f32[8,66,1]{2,1,0:T(8,128)S(1)} %get-tuple-element.945), channel_id=1, source_target_pairs={{1,0},{2,1},{3,2},{5,4},{6,5},{7,6},{9,8},{10,9},{11,10},{13,12},{... | collective-permute-start | bytes 6344 | tf_op jit(solution)/shard_map/ppermute | solution.py:20
  478.1 7.8 collective-permute-start.50
  480.0 9.9 collective-permute-start.51
  500.0 41.8 %collective-permute-start.54 = (f32[8,66,1]{2,1,0:T(8,128)S(1)}, f32[8,66,1]{2,1,0:T(8,128)S(1)}, u32[]{:S(2)}, u32[]{:S(2)}) collective-permute-start(f32[8,66,1]{2,1,0:T(8,128)S(1)} %get-tuple-element.942), channel_id=1, source_target_pairs={{0,1},{1,2},{2,3},{4,5},{5,6},{6,7},{8,9},{9,10},{10,11},{12,13},{... | collective-permute-start | bytes 6344 | tf_op jit(solution)/shard_map/ppermute | solution.py:18
  501.9 39.9 %collective-permute-start.55 = (f32[8,66,1]{2,1,0:T(8,128)S(1)}, f32[8,66,1]{2,1,0:T(8,128)S(1)}, u32[]{:S(2)}, u32[]{:S(2)}) collective-permute-start(f32[8,66,1]{2,1,0:T(8,128)S(1)} %get-tuple-element.941), channel_id=1, source_target_pairs={{1,0},{2,1},{3,2},{5,4},{6,5},{7,6},{9,8},{10,9},{11,10},{13,12},{... | collective-permute-start | bytes 6344 | tf_op jit(solution)/shard_map/ppermute | solution.py:20
  527.0 24.4 %all-to-all-start.5 = ((f32[128,1,32]{2,1,0:T(1,128)}), f32[128,1,32]{2,1,0:T(1,128)S(1)}, u32[]{:S(2)}, u32[]{:S(2)}) async-start(f32[128,1,32]{2,1,0:T(1,128)} %bitcast.20), calls=%async_computation.5 | async-start | bytes 131072 | tf_op jit(solution)/shard_map/all_to_all | solution.py:119
  573.0 13.9 %all-to-all-start.6 = ((f32[128,1,32]{2,1,0:T(1,128)}), f32[128,1,32]{2,1,0:T(1,128)S(1)}, u32[]{:S(2)}, u32[]{:S(2)}) async-start(f32[128,1,32]{2,1,0:T(1,128)} %bitcast.21), calls=%async_computation.6 | async-start | bytes 131072 | tf_op jit(solution)/shard_map/all_to_all | solution.py:109
  618.8 8.3 collective-permute-start.58
  620.9 10.0 collective-permute-start.59
  639.7 10.3 %collective-permute-start.62 = (f32[8,66,1]{2,1,0:T(8,128)S(1)}, f32[8,66,1]{2,1,0:T(8,128)S(1)}, u32[]{:S(2)}, u32[]{:S(2)}) collective-permute-start(f32[8,66,1]{2,1,0:T(8,128)S(1)} %get-tuple-element.938), channel_id=1, source_target_pairs={{0,1},{1,2},{2,3},{4,5},{5,6},{6,7},{8,9},{9,10},{10,11},{12,13},{... | collective-permute-start | bytes 6344 | tf_op jit(solution)/shard_map/ppermute | solution.py:18
  643.5 10.7 %collective-permute-start.63 = (f32[8,66,1]{2,1,0:T(8,128)S(1)}, f32[8,66,1]{2,1,0:T(8,128)S(1)}, u32[]{:S(2)}, u32[]{:S(2)}) collective-permute-start(f32[8,66,1]{2,1,0:T(8,128)S(1)} %get-tuple-element.937), channel_id=1, source_target_pairs={{1,0},{2,1},{3,2},{5,4},{6,5},{7,6},{9,8},{10,9},{11,10},{13,12},{... | collective-permute-start | bytes 6344 | tf_op jit(solution)/shard_map/ppermute | solution.py:20
  662.5 10.3 %collective-permute-start.66 = (f32[8,66,1]{2,1,0:T(8,128)S(1)}, f32[8,66,1]{2,1,0:T(8,128)S(1)}, u32[]{:S(2)}, u32[]{:S(2)}) collective-permute-start(f32[8,66,1]{2,1,0:T(8,128)S(1)} %get-tuple-element.936), channel_id=1, source_target_pairs={{0,1},{1,2},{2,3},{4,5},{5,6},{6,7},{8,9},{9,10},{10,11},{12,13},{... | collective-permute-start | bytes 6344 | tf_op jit(solution)/shard_map/ppermute | solution.py:18
  666.2 10.9 %collective-permute-start.67 = (f32[8,66,1]{2,1,0:T(8,128)S(1)}, f32[8,66,1]{2,1,0:T(8,128)S(1)}, u32[]{:S(2)}, u32[]{:S(2)}) collective-permute-start(f32[8,66,1]{2,1,0:T(8,128)S(1)} %get-tuple-element.935), channel_id=1, source_target_pairs={{1,0},{2,1},{3,2},{5,4},{6,5},{7,6},{9,8},{10,9},{11,10},{13,12},{... | collective-permute-start | bytes 6344 | tf_op jit(solution)/shard_map/ppermute | solution.py:20
  685.4 8.0 collective-permute-start.70
  686.9 10.9 %collective-permute-start.71 = (f32[8,66,1]{2,1,0:T(8,128)S(1)}, f32[8,66,1]{2,1,0:T(8,128)S(1)}, u32[]{:S(2)}, u32[]{:S(2)}) collective-permute-start(f32[8,66,1]{2,1,0:T(8,128)S(1)} %get-tuple-element.933), channel_id=1, source_target_pairs={{1,0},{2,1},{3,2},{5,4},{6,5},{7,6},{9,8},{10,9},{11,10},{13,12},{... | collective-permute-start | bytes 6344 | tf_op jit(solution)/shard_map/ppermute | solution.py:20
  706.1 7.8 collective-permute-start.74
  708.1 9.9 collective-permute-start.75
  728.0 41.5 %collective-permute-start.78 = (f32[8,66,1]{2,1,0:T(8,128)S(1)}, f32[8,66,1]{2,1,0:T(8,128)S(1)}, u32[]{:S(2)}, u32[]{:S(2)}) collective-permute-start(f32[8,66,1]{2,1,0:T(8,128)S(1)} %get-tuple-element.930), channel_id=1, source_target_pairs={{0,1},{1,2},{2,3},{4,5},{5,6},{6,7},{8,9},{9,10},{10,11},{12,13},{... | collective-permute-start | bytes 6344 | tf_op jit(solution)/shard_map/ppermute | solution.py:18
  730.0 39.6 %collective-permute-start.79 = (f32[8,66,1]{2,1,0:T(8,128)S(1)}, f32[8,66,1]{2,1,0:T(8,128)S(1)}, u32[]{:S(2)}, u32[]{:S(2)}) collective-permute-start(f32[8,66,1]{2,1,0:T(8,128)S(1)} %get-tuple-element.929), channel_id=1, source_target_pairs={{1,0},{2,1},{3,2},{5,4},{6,5},{7,6},{9,8},{10,9},{11,10},{13,12},{... | collective-permute-start | bytes 6344 | tf_op jit(solution)/shard_map/ppermute | solution.py:20
  755.0 24.2 %all-to-all-start.7 = ((f32[128,1,32]{2,1,0:T(1,128)}), f32[128,1,32]{2,1,0:T(1,128)S(1)}, u32[]{:S(2)}, u32[]{:S(2)}) async-start(f32[128,1,32]{2,1,0:T(1,128)} %bitcast.24), calls=%async_computation.7 | async-start | bytes 131072 | tf_op jit(solution)/shard_map/all_to_all | solution.py:119
  800.8 14.4 %all-to-all-start.8 = ((f32[128,1,32]{2,1,0:T(1,128)}), f32[128,1,32]{2,1,0:T(1,128)S(1)}, u32[]{:S(2)}, u32[]{:S(2)}) async-start(f32[128,1,32]{2,1,0:T(1,128)} %bitcast.25), calls=%async_computation.8 | async-start | bytes 131072 | tf_op jit(solution)/shard_map/all_to_all | solution.py:109
  847.1 8.3 collective-permute-start.82
  849.2 10.0 collective-permute-start.83
  868.0 10.3 %collective-permute-start.86 = (f32[8,66,1]{2,1,0:T(8,128)S(1)}, f32[8,66,1]{2,1,0:T(8,128)S(1)}, u32[]{:S(2)}, u32[]{:S(2)}) collective-permute-start(f32[8,66,1]{2,1,0:T(8,128)S(1)} %get-tuple-element.926), channel_id=1, source_target_pairs={{0,1},{1,2},{2,3},{4,5},{5,6},{6,7},{8,9},{9,10},{10,11},{12,13},{... | collective-permute-start | bytes 6344 | tf_op jit(solution)/shard_map/ppermute | solution.py:18
  871.8 10.7 %collective-permute-start.87 = (f32[8,66,1]{2,1,0:T(8,128)S(1)}, f32[8,66,1]{2,1,0:T(8,128)S(1)}, u32[]{:S(2)}, u32[]{:S(2)}) collective-permute-start(f32[8,66,1]{2,1,0:T(8,128)S(1)} %get-tuple-element.925), channel_id=1, source_target_pairs={{1,0},{2,1},{3,2},{5,4},{6,5},{7,6},{9,8},{10,9},{11,10},{13,12},{... | collective-permute-start | bytes 6344 | tf_op jit(solution)/shard_map/ppermute | solution.py:20
  890.8 10.3 %collective-permute-start.90 = (f32[8,66,1]{2,1,0:T(8,128)S(1)}, f32[8,66,1]{2,1,0:T(8,128)S(1)}, u32[]{:S(2)}, u32[]{:S(2)}) collective-permute-start(f32[8,66,1]{2,1,0:T(8,128)S(1)} %get-tuple-element.924), channel_id=1, source_target_pairs={{0,1},{1,2},{2,3},{4,5},{5,6},{6,7},{8,9},{9,10},{10,11},{12,13},{... | collective-permute-start | bytes 6344 | tf_op jit(solution)/shard_map/ppermute | solution.py:18
  894.5 10.9 %collective-permute-start.91 = (f32[8,66,1]{2,1,0:T(8,128)S(1)}, f32[8,66,1]{2,1,0:T(8,128)S(1)}, u32[]{:S(2)}, u32[]{:S(2)}) collective-permute-start(f32[8,66,1]{2,1,0:T(8,128)S(1)} %get-tuple-element.923), channel_id=1, source_target_pairs={{1,0},{2,1},{3,2},{5,4},{6,5},{7,6},{9,8},{10,9},{11,10},{13,12},{... | collective-permute-start | bytes 6344 | tf_op jit(solution)/shard_map/ppermute | solution.py:20
  913.7 8.0 collective-permute-start.94
  915.2 10.9 %collective-permute-start.95 = (f32[8,66,1]{2,1,0:T(8,128)S(1)}, f32[8,66,1]{2,1,0:T(8,128)S(1)}, u32[]{:S(2)}, u32[]{:S(2)}) collective-permute-start(f32[8,66,1]{2,1,0:T(8,128)S(1)} %get-tuple-element.921), channel_id=1, source_target_pairs={{1,0},{2,1},{3,2},{5,4},{6,5},{7,6},{9,8},{10,9},{11,10},{13,12},{... | collective-permute-start | bytes 6344 | tf_op jit(solution)/shard_map/ppermute | solution.py:20
  934.4 7.8 collective-permute-start.98
  936.4 9.9 collective-permute-start.99
  (59 other events, 801.2 us)
where the time goes:
time: 1020 us; the launch traced here: 1010 us
  starting transfers between devices  340 us (33%)
  waiting for transfers between devices  268 us (26%)
  local copies, waits for them, and re-layouts  204 us (20%)
  other arithmetic  167 us (16%)
  blocking collectives  21 us (2%)
    ppermute x50, starting transfers between devices, extended(): lax.ppermute(tail, axis, [(i, (i + 1) % count) for i in range(ends)])  148 us
    ppermute x50, waiting for transfers between devices, extended(): lax.ppermute(tail, axis, [(i, (i + 1) % count) for i in range(ends)])  117 us
    ppermute x50, starting transfers between devices, extended(): lax.ppermute(head, axis, [((i + 1) % count, i) for i in range(ends)])  107 us
    gather x4, local copies, waits for them, and re-layouts, shards(): wall_slots = temp[0].reshape(-1)[cell_recv].reshape(devices, cap)  92.1 us
    scatter-add x4, other arithmetic, shards(): jax.ops.segment_sum(htc_recv * tf_recv, cell_recv, num_segments=surface)  91.5 us
    ppermute x50, waiting for transfers between devices, extended(): lax.ppermute(head, axis, [((i + 1) % count, i) for i in range(ends)])  83.5 us
    scatter x6, local copies, waits for them, and re-layouts, pack(): jnp.zeros((devices * cap,), values.dtype).at[slot].set(values, mode='drop')  49.3 us
    gather x4, local copies, waits for them, and re-layouts, shards(): wall_face = jnp.take(wall_back.reshape(-1), safe_slot)  47.1 us
  transfers between devices with their start and end apart: 109, of which 71 were waited for; matrix products, arithmetic and copies ran while one was open for 11% of the time, Pallas kernels for 0%

commit v1 on v0

v1 whole, which is shorter than its diff:
```python
import functools

import jax
import jax.numpy as jnp
from jax import lax
from jax.experimental import pallas as pl
from jax.experimental.pallas import tpu as pltpu
from jax.sharding import PartitionSpec as P

SWEEPS = 6
SUBITERS = 4
HALO = SWEEPS * SUBITERS
LANES = 128
FIELDS = 2 * SUBITERS
CHUNK = 8
MESH = pl.DeviceIdType.MESH
f32 = jnp.float32
bf16 = jnp.bfloat16


def iota(shape, dim):
    return lax.broadcasted_iota(jnp.int32, shape, dim)


def split(value, parts):
    pieces = []
    for _ in range(parts):
        piece = value.astype(bf16)
        pieces.append(piece)
        value = value - piece.astype(f32)
    return pieces


def nt(a, b):
    return lax.dot_general(a, b, (((1,), (1,)), ((), ())), preferred_element_type=f32)


def nn(a, b):
    return jnp.dot(a, b, preferred_element_type=f32)


def kernel(
    n_blade,
    n_span,
    cap,
    solid_ref,
    kappa_ref,
    cool_ref,
    fluid_ref,
    htc_ref,
    dest_ref,
    cell_ref,
    count_ref,
    solid_out,
    fluid_out,
    flux_out,
    ext_t,
    ext_k,
    ext_c,
    ext_f,
    acc,
    temp_a,
    temp_b,
    kappa,
    cool,
    fields,
    numer_add,
    denom_add,
    tw,
    owner,
    rank,
    send_fwd,
    recv_fwd,
    send_back,
    recv_back,
    slot_x,
    slot_s,
    slot_v,
    pick_s,
    wall,
    local_sem,
    halo_send,
    halo_recv,
    face_send,
    face_recv,
):
    devices = n_blade * n_span
    layers, cells_x, cells_s = solid_ref.shape
    blocks = fluid_ref.shape[0]
    ib, js = lax.axis_index("blade"), lax.axis_index("span")
    me = ib * n_span + js
    lo, hi = HALO, HALO + cells_x
    rows = cells_s + 2 * HALO

    barrier = pltpu.get_barrier_semaphore()

    def place(k):
        peer = lax.rem(me + k, devices)
        return peer, (peer // n_span, lax.rem(peer, n_span))

    @pl.loop(1, devices)
    def _(k):
        _, at = place(k)
        pl.semaphore_signal(barrier, inc=1, device_id=at, device_id_type=MESH)

    inner_t = pltpu.make_async_copy(solid_ref, ext_t.at[:, lo:hi, :], local_sem.at[0])
    inner_k = pltpu.make_async_copy(kappa_ref, ext_k.at[:, lo:hi, :], local_sem.at[1])
    inner_t.start()
    inner_k.start()

    number = iota((blocks, LANES), 0) * LANES + iota((blocks, LANES), 1)
    live = number < jnp.broadcast_to(count_ref[...], (blocks, LANES))
    owner_row = jnp.where(live, dest_ref[...], -1)
    before = (iota((LANES, 2 * LANES), 0) < iota((LANES, 2 * LANES), 1)) | (
        iota((LANES, 2 * LANES), 1) >= LANES
    )
    before = before.astype(f32).astype(bf16)
    dev_iota = iota((LANES, LANES), 0)
    offset = jnp.zeros((LANES, LANES), f32)
    packed = jnp.zeros((LANES, LANES), f32)
    cell_f = cell_ref[...].astype(f32)
    slot_iota = iota((cap, LANES), 0).astype(f32)
    for b in range(blocks):
        mine = jnp.where(dev_iota == owner_row[b : b + 1, :], 1.0, 0.0)
        mine_b = mine.astype(bf16)
        owner[:, b * LANES : (b + 1) * LANES] = mine_b
        counts = nn(mine_b, before)
        order = jnp.sum(mine * (counts[:, :LANES] + offset), axis=0, keepdims=True)
        offset = offset + counts[:, LANES:]
        rank[b : b + 1, :] = order
        at_slot = slot_iota == order
        spread = jnp.concatenate(
            [
                jnp.where(at_slot, row[b : b + 1, :], 0.0)
                for row in (htc_ref[...], fluid_ref[...], cell_f)
            ]
            + [jnp.zeros((LANES - 3 * cap, LANES), f32)],
            axis=0,
        )
        for piece in split(spread, 3):
            packed = packed + nt(mine_b, piece)
    send_fwd[...] = packed.reshape(LANES, 1, LANES)
    if devices < LANES:
        recv_fwd[...] = jnp.zeros_like(recv_fwd)
        recv_back[...] = jnp.zeros_like(recv_back)

    pl.semaphore_wait(barrier, devices - 1)

    west = (lax.rem(ib + n_blade - 1, n_blade), js)
    east = (lax.rem(ib + 1, n_blade), js)
    south = (ib, lax.rem(js + n_span - 1, n_span))
    north = (ib, lax.rem(js + 1, n_span))

    def remote(src, dst, sem, to):
        return pltpu.make_async_remote_copy(
            src_ref=src,
            dst_ref=dst,
            send_sem=halo_send.at[sem],
            recv_sem=halo_recv.at[sem],
            device_id=to,
            device_id_type=MESH,
        )

    def across_blade(src, first, last, ext, sem):
        return (
            remote(src.at[..., first : first + HALO, :], ext.at[..., hi : hi + HALO, :], sem, west),
            remote(src.at[..., last - HALO : last, :], ext.at[..., 0:HALO, :], sem + 1, east),
        )

    x_halos = (
        across_blade(solid_ref, 0, cells_x, ext_t, 0)
        + across_blade(kappa_ref, 0, cells_x, ext_k, 2)
        + across_blade(cool_ref, 0, cells_x, ext_c, 4)
    )
    for copy in x_halos:
        copy.start()

    def exchange(send, recv, which):
        @pl.loop(1, devices)
        def _(k):
            peer, at = place(k)
            pltpu.make_async_remote_copy(
                src_ref=send.at[peer],
                dst_ref=recv.at[me],
                send_sem=face_send.at[which],
                recv_sem=face_recv.at[which],
                device_id=at,
                device_id_type=MESH,
            ).start()

        recv[pl.ds(me, 1)] = send[pl.ds(me, 1)]

    def arrived(send, recv, which):
        whole = pltpu.make_async_remote_copy(
            src_ref=send.at[pl.ds(0, devices - 1)],
            dst_ref=recv.at[pl.ds(0, devices - 1)],
            send_sem=face_send.at[which],
            recv_sem=face_recv.at[which],
            device_id=east,
            device_id_type=MESH,
        )
        whole.wait_send()
        whole.wait_recv()

    exchange(send_fwd, recv_fwd, 0)

    ext_c[lo:hi, :] = cool_ref[...]
    numer_add[...] = jnp.zeros_like(numer_add)
    denom_add[...] = jnp.zeros_like(denom_add)
    inner_t.wait()
    inner_k.wait()
    for copy in x_halos:
        copy.wait()
    for l in range(layers):
        temp_a[pl.ds(lo * 8 + l, cells_s, stride=8), :] = 0.5 * ext_t[l].T
        kappa[pl.ds(lo * 8 + l, cells_s, stride=8), :] = ext_k[l].T
    cool[lo : lo + cells_s, :] = ext_c[...].T

    def across_span(ref, unit, sem):
        first, last = lo * unit, (lo + cells_s) * unit
        width = HALO * unit

        def part(start):
            if len(ref.shape) == 3:
                return ref.at[:, start : start + width, :]
            return ref.at[start : start + width, :]

        return (
            remote(part(first), part(last), sem, south),
            remote(part(last - width), part(0), sem + 1, north),
        )

    s_halos = across_span(temp_a, 8, 6) + across_span(kappa, 8, 8) + across_span(cool, 1, 10)
    for copy in s_halos:
        copy.start()

    arrived(send_fwd, recv_fwd, 0)
    got = recv_fwd[...].reshape(LANES, LANES).T
    h = got[0:cap]
    tf = got[cap : 2 * cap]
    cell = got[2 * cap : 3 * cap].astype(jnp.int32)
    slot_x[...] = cell // cells_s
    slot_s[...] = cell % cells_s
    inv = 1.0 / (h + 2.0)
    keep = 2.0 * inv
    value = 0.5 * h
    slot_v[0] = value
    value = 0.25 * h * tf
    for n in range(SUBITERS):
        slot_v[1 + n] = value
        value = value * keep
    value = 0.5 * h * (h * inv)
    for n in range(SUBITERS - 1):
        slot_v[1 + SUBITERS + n] = value
        value = value * keep
    acc[...] = jnp.zeros_like(acc)
    x_iota = iota((cells_x, LANES), 0)
    s_iota = iota((cells_s, LANES), 0)

    group = 4

    @pl.loop(0, cap // group)
    def _(g):
        lhs, rhs = [], []
        for j in range(group):
            r = g * group + j
            row = pl.ds(r, 1)
            s_hit = jnp.where(s_iota == slot_s[row, :], 1.0, 0.0).astype(bf16)
            pick_s[:, pl.ds(pl.multiple_of(r * LANES, LANES), LANES)] = s_hit
            x_hit = x_iota == slot_x[row, :]
            upper, lower = [], []
            for k in range(FIELDS):
                v = slot_v[k, row, :]
                v_up = v.astype(bf16).astype(f32)
                upper.append(jnp.where(x_hit, v_up, 0.0).astype(bf16))
                lower.append(jnp.where(x_hit, v - v_up, 0.0).astype(bf16))
            lhs += [jnp.concatenate(upper, axis=0), jnp.concatenate(lower, axis=0)]
            rhs += [s_hit, s_hit]
        acc[...] += nt(jnp.concatenate(lhs, axis=1), jnp.concatenate(rhs, axis=1))

    for k in range(FIELDS):
        ext_f[k, lo:hi, :] = acc[k * cells_x : (k + 1) * cells_x, :]

    f_x = across_blade(ext_f, lo, hi, ext_f, 12)
    for copy in f_x:
        copy.start()

    for copy in s_halos:
        copy.wait()
    lane = iota((8, LANES), 1)
    inside_x = ((lane >= lo) | (ib > 0)) & ((lane < hi) | (ib < n_blade - 1))

    @pl.loop(0, rows)
    def _(s):
        inside = inside_x & (((s >= lo) | (js > 0)) & ((s < lo + cells_s) | (js < n_span - 1)))
        at = pl.ds(pl.multiple_of(s * 8, 8), 8)
        kappa[at, :] = jnp.where(inside, kappa[at, :], 1e-15)

    for copy in f_x:
        copy.wait()
    for k in range(FIELDS):
        fields[k, lo : lo + cells_s, :] = ext_f[k].T
    f_s = across_span(fields, 1, 14)
    for copy in f_s:
        copy.start()
    for copy in f_s:
        copy.wait()

    every = pl.ds(0, rows, stride=8)
    denom_add[every, :] = fields[0]
    denom_add[pl.ds(layers - 1, rows, stride=8), :] = 0.5 * cool[...]
    not_last = jnp.where(iota((8, LANES), 0) < layers - 1, 1.0, 0.0)

    def conduct(t, k):
        return k + k * (t * t)

    def weight(a, b):
        return a * b / (a + b)

    def sweep(src, dst, step):
        first = step + 1

        def tile(ref, s):
            return ref[pl.ds(pl.multiple_of(s * 8, 8), 8), :]

        def chunk(i, carry):
            t_prev, t_here, c_here, w_prev = carry
            for j in range(CHUNK):
                s = first + i * CHUNK + j
                t_next = tile(src, s + 1)
                c_next = conduct(t_next, tile(kappa, s + 1))
                w_next = weight(c_here, c_next)
                w_up = weight(c_here, pltpu.roll(c_here, LANES - 1, 1))
                w_down = pltpu.roll(w_up, 1, 1)
                w_in = weight(c_here, pltpu.roll(c_here, 7, 0)) * not_last
                w_out = pltpu.roll(w_in, 1, 0)
                numer = (
                    (w_next * t_next + w_prev * t_prev)
                    + (w_up * pltpu.roll(t_here, LANES - 1, 1) + w_down * pltpu.roll(t_here, 1, 1))
                    + (w_in * pltpu.roll(t_here, 7, 0) + w_out * pltpu.roll(t_here, 1, 0))
                    + tile(numer_add, s)
                )
                denom = ((w_next + w_prev) + (w_up + w_down)) + (
                    (w_in + w_out) + tile(denom_add, s)
                )
                dst[pl.ds(pl.multiple_of(s * 8, 8), 8), :] = numer / denom
                t_prev, t_here, c_here, w_prev = t_here, t_next, c_next, w_next
            return t_prev, t_here, c_here, w_prev

        t_prev, t_here = tile(src, first - 1), tile(src, first)
        c_prev = conduct(t_prev, tile(kappa, first - 1))
        c_here = conduct(t_here, tile(kappa, first))
        count = (rows - 2 * first + CHUNK - 1) // CHUNK
        lax.fori_loop(0, count, chunk, (t_prev, t_here, c_here, weight(c_prev, c_here)))

    for n in range(SUBITERS):
        extra = fields[1 + n]
        for m in range(n):
            extra = extra + tw[m] * fields[SUBITERS + n - m]
        numer_add[every, :] = extra

        @pl.loop(0, SWEEPS // 2)
        def _(p):
            step = n * SWEEPS + 2 * p
            sweep(temp_a, temp_b, step)
            sweep(temp_b, temp_a, step + 1)

        now = temp_a[every, :]
        tw[n] = now
        rows_x = now[lo : lo + cells_s, :].T[lo:hi, :]
        up, low = split(rows_x, 2)
        wall[2 * n * cells_x : (2 * n + 1) * cells_x, :] = up
        wall[(2 * n + 1) * cells_x : (2 * n + 2) * cells_x, :] = low

    @pl.loop(0, cap)
    def _(r):
        row = pl.ds(r, 1)
        lanes = pl.ds(pl.multiple_of(r * LANES, LANES), LANES)
        found = nn(wall[...], pick_s[:, lanes])
        x_hit = x_iota == slot_x[row, :]
        for n in range(SUBITERS):
            both = (
                found[2 * n * cells_x : (2 * n + 1) * cells_x]
                + found[(2 * n + 1) * cells_x : (2 * n + 2) * cells_x]
            )
            slot_v[n, row, :] = jnp.sum(jnp.where(x_hit, both, 0.0), axis=0, keepdims=True)

    got = recv_fwd[...].reshape(LANES, LANES).T
    h = got[0:cap]
    tf = got[cap : 2 * cap]
    inv = 1.0 / (h + 2.0)
    for n in range(SUBITERS):
        q = h * (tf - 2.0 * slot_v[n])
        tf = tf - q * inv
    back = jnp.concatenate([q, tf, jnp.zeros((LANES - 2 * cap, LANES), f32)], axis=0)
    send_back[...] = back.T.reshape(LANES, 1, LANES)
    exchange(send_back, recv_back, 1)

    for l in range(layers):
        final = temp_a[pl.ds(lo * 8 + l, cells_s, stride=8), :]
        solid_out[l] = 2.0 * final.T[lo:hi, :]

    arrived(send_back, recv_back, 1)
    table = recv_back[...].reshape(LANES, LANES).T[0 : 2 * cap]
    pieces = jnp.concatenate(split(table, 3), axis=0)
    for b in range(blocks):
        seen = nn(pieces, owner[:, b * LANES : (b + 1) * LANES])
        seen = seen[0 : 2 * cap] + seen[2 * cap : 4 * cap] + seen[4 * cap : 6 * cap]
        at_slot = slot_iota == rank[b : b + 1, :]
        q_row = jnp.sum(jnp.where(at_slot, seen[0:cap], 0.0), axis=0, keepdims=True)
        t_row = jnp.sum(jnp.where(at_slot, seen[cap : 2 * cap], 0.0), axis=0, keepdims=True)
        on = live[b : b + 1, :]
        flux_out[b : b + 1, :] = jnp.where(on, q_row, 0.0)
        fluid_out[b : b + 1, :] = jnp.where(on, t_row, fluid_ref[b : b + 1, :])


def shards(
    n_blade,
    n_span,
    solid_temp,
    base_conductivity,
    coolant_htc,
    fluid_temp,
    wall_htc,
    face_dest,
    face_cell,
    face_count,
):
    layers, cells_x, cells_s = solid_temp.shape
    slots = fluid_temp.shape[0]
    cap = 32
    blocks = slots // LANES
    rows = cells_s + 2 * HALO
    tall = rows + CHUNK
    vmem = pl.BlockSpec(memory_space=pltpu.VMEM)
    hbm = pl.BlockSpec(memory_space=pl.ANY)
    big = pltpu.VMEM((tall * 8, LANES), f32)
    faces = pltpu.VMEM((LANES, 1, LANES), f32)
    ext = pltpu.VMEM((layers, LANES, cells_s), f32)
    temp, fluid, flux = pl.pallas_call(
        functools.partial(kernel, n_blade, n_span, cap),
        out_shape=(
            jax.ShapeDtypeStruct(solid_temp.shape, f32),
            jax.ShapeDtypeStruct((blocks, LANES), f32),
            jax.ShapeDtypeStruct((blocks, LANES), f32),
        ),
        in_specs=[hbm, hbm, vmem, vmem, vmem, vmem, vmem, vmem],
        out_specs=(vmem, vmem, vmem),
        scratch_shapes=[
            ext,
            ext,
            pltpu.VMEM((LANES, cells_s), f32),
            ext,
            pltpu.VMEM((FIELDS * cells_x, cells_s), f32),
            big,
            big,
            big,
            pltpu.VMEM((rows, LANES), f32),
            pltpu.VMEM((FIELDS, rows, LANES), f32),
            big,
            big,
            pltpu.VMEM((SUBITERS, rows, LANES), f32),
            pltpu.VMEM((LANES, slots), bf16),
            pltpu.VMEM((blocks, LANES), f32),
            faces,
            faces,
            faces,
            faces,
            pltpu.VMEM((cap, LANES), jnp.int32),
            pltpu.VMEM((cap, LANES), jnp.int32),
            pltpu.VMEM((FIELDS, cap, LANES), f32),
            pltpu.VMEM((cells_s, cap * LANES), bf16),
            pltpu.VMEM((2 * SUBITERS * cells_x, cells_s), bf16),
            pltpu.SemaphoreType.DMA((2,)),
            pltpu.SemaphoreType.DMA((16,)),
            pltpu.SemaphoreType.DMA((16,)),
            pltpu.SemaphoreType.DMA((2,)),
            pltpu.SemaphoreType.DMA((2,)),
        ],
        compiler_params=pltpu.CompilerParams(
            collective_id=0, has_side_effects=True, vmem_limit_bytes=48 << 20
        ),
    )(
        solid_temp,
        base_conductivity,
        coolant_htc,
        fluid_temp.reshape(blocks, LANES),
        wall_htc.reshape(blocks, LANES),
        face_dest.reshape(blocks, LANES),
        face_cell.reshape(blocks, LANES),
        face_count.reshape(1, 1),
    )
    return temp, fluid.reshape(slots), flux.reshape(slots)


def solution(mesh):
    placed = (
        P(None, "blade", "span"),
        P(None, "blade", "span"),
        P("blade", "span"),
        P(("blade", "span")),
        P(("blade", "span")),
        P(("blade", "span"), None),
        P(("blade", "span")),
        P(("blade", "span")),
    )
    return jax.shard_map(
        functools.partial(shards, mesh.shape["blade"], mesh.shape["span"]),
        mesh=mesh,
        in_specs=placed,
        out_specs=(P(None, "blade", "span"), P(("blade", "span")), P(("blade", "span"))),
        check_vma=False,
    )
```

time: 1020 us -> 130 us (0.13); the launches traced: 1010 us -> 130 us
  starting transfers between devices: 340 us -> 0 us
  waiting for transfers between devices: 268 us -> 0 us
  local copies, waits for them, and re-layouts: 204 us -> 6.68 us
  other arithmetic: 167 us -> 0 us
  Pallas kernels: 0 us -> 122 us
  blocking collectives: 21 us -> 0 us
    ppermute x100 -> x0, starting transfers between devices: 255 us -> none  [the longest x50 148 us: extended(): lax.ppermute(tail, axis, [(i, (i + 1) % count) for i in range(ends)])]
    ppermute x100 -> x0, waiting for transfers between devices: 200 us -> none  [the longest x50 117 us: extended(): lax.ppermute(tail, axis, [(i, (i + 1) % count) for i in range(ends)])]
    gather x8 -> x0, local copies, waits for them, and re-layouts: 139 us -> none  [the longest x4 92.1 us: shards(): wall_slots = temp[0].reshape(-1)[cell_recv].reshape(devices, cap)]
    pallas_call x0 -> x1, Pallas kernels: none -> 122 us  [shards(): pl.pallas_call(functools.partial(kernel, n_blade, n_span, cap), out_shape...]
    scatter-add x76 -> x0, other arithmetic: 115 us -> none  [the longest x4 91.5 us: shards(): jax.ops.segment_sum(htc_recv * tf_recv, cell_recv, num_segments=surface)]
    all_to_all x9 -> x0, starting transfers between devices: 85.1 us -> none  [the longest x3 43.9 us: shards(): lax.all_to_all(wall_slots, ('blade', 'span'), split_axis=0, concat_axis=0...]
    all_to_all x9 -> x0, waiting for transfers between devices: 67.7 us -> none  [the longest x4 35.2 us: shards(): lax.all_to_all(pack(tf), ('blade', 'span'), split_axis=0, concat_axis=0,...]
    scatter x6 -> x0, local copies, waits for them, and re-layouts: 49.3 us -> none  [pack(): jnp.zeros((devices * cap,), values.dtype).at[slot].set(values, mode='drop')]
  transfers between devices with their start and end apart: 109 -> 0, of which waited for: 71 -> 0; matrix products, arithmetic and copies ran while one was open for 11% -> 0% of each run, Pallas kernels for 0% -> 0%
where the time goes in v1:
time: 130 us
  Pallas kernels  122 us (94%)
  local copies, waits for them, and re-layouts  6.68 us (5%)
  between operations  1.32 us (1%)
    pallas_call x1, Pallas kernels, shards(): pl.pallas_call(functools.partial(kernel, n_blade, n_span, cap), out_shape...  122 us
    unnamed x17, local copies, waits for them, and re-layouts  6.68 us

profile of v1, /device:TPU:1, one launch (start us, length us, event | category | flops | bytes accessed | tf_op | source)
XLA Modules:
  0.0 129.9 jit_solution(11905576382953378645)
XLA Ops:
  0.6 0.0 copy-start.3
  1.3 0.0 copy-done.3
  1.3 0.0 copy-start
  1.3 0.9 copy-done
  2.3 0.0 copy-start.1
  2.3 0.9 copy-done.1
  3.2 0.0 copy-start.2
  3.2 0.8 copy-done.2
  4.0 0.0 copy-start.4
  4.0 0.7 copy-done.4
  4.7 0.0 copy-start.5
  4.7 0.7 copy-done.5
  5.4 0.0 copy-start.6
  5.4 0.7 copy-done.6
  6.1 121.9 %shard_map.103 = (f32[8,64,128]{2,1,0:T(8,128)S(1)}, f32[16,128]{1,0:T(8,128)S(1)}, f32[16,128]{1,0:T(8,128)S(1)}) custom-call(f32[8,64,128]{2,1,0:T(8,128)S(1)} %copy-done, f32[8,64,128]{2,1,0:T(8,128)S(1)} %copy-done.1, f32[64,128]{1,0:T(8,128)S(1)} %copy-done.2, f32[16,128]{1,0:T(8,128)S(1)} %bitcast.8, f32[16,128]{1,0:T(8,128)S(1)} %bitcast.9, ...), custom_call_target="tpu_custom_call" | custom-call | tf_op jit(solution)/shard_map/pallas_call | solution.py:440
  128.0 0.7 copy.15
  128.7 0.6 copy.16
  129.3 0.6 copy.17
Async XLA Ops:
  0.6 0.7 copy-start.3
  1.3 0.9 copy-start
  2.3 0.9 copy-start.1
  3.2 0.8 copy-start.2
  4.0 0.7 copy-start.4
  4.7 0.7 copy-start.5
  5.4 0.7 copy-start.6

commit v2 on v1

--- a/solution.py
+++ b/solution.py
@@ -12,7 +12,9 @@
 HALO = SWEEPS * SUBITERS
 LANES = 128
 FIELDS = 2 * SUBITERS
-CHUNK = 8
+PIECES = 3
+CHUNK = 16
+PAD = 16
 MESH = pl.DeviceIdType.MESH
 f32 = jnp.float32
 bf16 = jnp.bfloat16
@@ -54,14 +56,20 @@
     solid_out,
     fluid_out,
     flux_out,
+    fluid,
+    htc,
+    dest,
+    cells,
     ext_t,
     ext_k,
     ext_c,
     ext_f,
     acc,
-    temp_a,
-    temp_b,
-    kappa,
+    state_a,
+    state_b,
+    rho,
+    rho_up,
+    rho_down,
     cool,
     fields,
     numer_add,
@@ -76,7 +84,7 @@
     slot_x,
     slot_s,
     slot_v,
-    pick_s,
+    pick,
     wall,
     local_sem,
     halo_send,
@@ -87,6 +95,7 @@
     devices = n_blade * n_span
     layers, cells_x, cells_s = solid_ref.shape
     blocks = fluid_ref.shape[0]
+    temp_a = state_a[0]
     ib, js = lax.axis_index("blade"), lax.axis_index("span")
     me = ib * n_span + js
     lo, hi = HALO, HALO + cells_x
@@ -94,23 +103,46 @@
 
     barrier = pltpu.get_barrier_semaphore()
 
-    def place(k):
+    loads = [
+        pltpu.make_async_copy(src, dst, local_sem.at[i])
+        for i, (src, dst) in enumerate(
+            (
+                (dest_ref, dest),
+                (cell_ref, cells),
+                (htc_ref, htc),
+                (fluid_ref, fluid),
+                (solid_ref, ext_t.at[:, lo:hi, :]),
+                (kappa_ref, ext_k.at[:, lo:hi, :]),
+                (cool_ref, ext_c.at[lo:hi, :]),
+            )
+        )
+    ]
+    for load in loads:
+        load.start()
+
+    def peers(visit):
+        unit = 7 if (devices - 1) % 7 == 1 else 1
+        if unit > 1:
+            visit_one(visit, devices - 1)
+
+        @pl.loop(0, (devices - 1) // unit)
+        def _(i):
+            for j in range(unit):
+                visit_one(visit, i * unit + j + 1)
+
+    def visit_one(visit, k):
         peer = lax.rem(me + k, devices)
-        return peer, (peer // n_span, lax.rem(peer, n_span))
-
-    @pl.loop(1, devices)
-    def _(k):
-        _, at = place(k)
-        pl.semaphore_signal(barrier, inc=1, device_id=at, device_id_type=MESH)
-
-    inner_t = pltpu.make_async_copy(solid_ref, ext_t.at[:, lo:hi, :], local_sem.at[0])
-    inner_k = pltpu.make_async_copy(kappa_ref, ext_k.at[:, lo:hi, :], local_sem.at[1])
-    inner_t.start()
-    inner_k.start()
+        visit(peer, (lax.div(peer, n_span), lax.rem(peer, n_span)))
+
+    peers(
+        lambda _, at: pl.semaphore_signal(barrier, inc=1, device_id=at, device_id_type=MESH)
+    )
+    for load in loads[:4]:
+        load.wait()
 
     number = iota((blocks, LANES), 0) * LANES + iota((blocks, LANES), 1)
     live = number < jnp.broadcast_to(count_ref[...], (blocks, LANES))
-    owner_row = jnp.where(live, dest_ref[...], -1)
+    owner_row = jnp.where(live, dest[...], -1)
     before = (iota((LANES, 2 * LANES), 0) < iota((LANES, 2 * LANES), 1)) | (
         iota((LANES, 2 * LANES), 1) >= LANES
     )
@@ -118,7 +150,7 @@
     dev_iota = iota((LANES, LANES), 0)
     offset = jnp.zeros((LANES, LANES), f32)
     packed = jnp.zeros((LANES, LANES), f32)
-    cell_f = cell_ref[...].astype(f32)
+    cell_f = cells[...].astype(f32)
     slot_iota = iota((cap, LANES), 0).astype(f32)
     for b in range(blocks):
         mine = jnp.where(dev_iota == owner_row[b : b + 1, :], 1.0, 0.0)
@@ -132,7 +164,7 @@
         spread = jnp.concatenate(
             [
                 jnp.where(at_slot, row[b : b + 1, :], 0.0)
-                for row in (htc_ref[...], fluid_ref[...], cell_f)
+                for row in (htc[...], fluid[...], cell_f)
             ]
             + [jnp.zeros((LANES - 3 * cap, LANES), f32)],
             axis=0,
@@ -176,10 +208,8 @@
         copy.start()
 
     def exchange(send, recv, which):
-        @pl.loop(1, devices)
-        def _(k):
-            peer, at = place(k)
-            pltpu.make_async_remote_copy(
+        peers(
+            lambda peer, at: pltpu.make_async_remote_copy(
                 src_ref=send.at[peer],
                 dst_ref=recv.at[me],
                 send_sem=face_send.at[which],
@@ -187,6 +217,7 @@
                 device_id=at,
                 device_id_type=MESH,
             ).start()
+        )
 
         recv[pl.ds(me, 1)] = send[pl.ds(me, 1)]
 
@@ -204,20 +235,20 @@
 
     exchange(send_fwd, recv_fwd, 0)
 
-    ext_c[lo:hi, :] = cool_ref[...]
     numer_add[...] = jnp.zeros_like(numer_add)
     denom_add[...] = jnp.zeros_like(denom_add)
-    inner_t.wait()
-    inner_k.wait()
+    for load in loads[4:]:
+        load.wait()
     for copy in x_halos:
         copy.wait()
     for l in range(layers):
-        temp_a[pl.ds(lo * 8 + l, cells_s, stride=8), :] = 0.5 * ext_t[l].T
-        kappa[pl.ds(lo * 8 + l, cells_s, stride=8), :] = ext_k[l].T
+        column = pl.ds((PAD + lo) * 8 + l, cells_s, stride=8)
+        temp_a[column, :] = 0.5 * ext_t[l].T
+        rho[column, :] = 1.0 / ext_k[l].T
     cool[lo : lo + cells_s, :] = ext_c[...].T
 
-    def across_span(ref, unit, sem):
-        first, last = lo * unit, (lo + cells_s) * unit
+    def across_span(ref, unit, pad, sem):
+        first, last = (pad + lo) * unit, (pad + lo + cells_s) * unit
         width = HALO * unit
 
         def part(start):
@@ -227,10 +258,14 @@
 
         return (
             remote(part(first), part(last), sem, south),
-            remote(part(last - width), part(0), sem + 1, north),
-        )
-
-    s_halos = across_span(temp_a, 8, 6) + across_span(kappa, 8, 8) + across_span(cool, 1, 10)
+            remote(part(last - width), part(pad * unit), sem + 1, north),
+        )
+
+    s_halos = (
+        across_span(temp_a, 8, PAD, 6)
+        + across_span(rho, 8, PAD, 8)
+        + across_span(cool, 1, 0, 10)
+    )
     for copy in s_halos:
         copy.start()
 
@@ -239,8 +274,9 @@
     h = got[0:cap]
     tf = got[cap : 2 * cap]
     cell = got[2 * cap : 3 * cap].astype(jnp.int32)
-    slot_x[...] = cell // cells_s
-    slot_s[...] = cell % cells_s
+    x_cell = cell // cells_s
+    slot_x[...] = x_cell // 2
+    slot_s[...] = cell - (x_cell // 2) * (2 * cells_s)
     inv = 1.0 / (h + 2.0)
     keep = 2.0 * inv
     value = 0.5 * h
@@ -254,9 +290,9 @@
         slot_v[1 + SUBITERS + n] = value
         value = value * keep
     acc[...] = jnp.zeros_like(acc)
-    x_iota = iota((cells_x, LANES), 0)
-    s_iota = iota((cells_s, LANES), 0)
-
+    half = cells_x // 2
+    x_iota = iota((half, LANES), 0)
+    s_iota = iota((2 * cells_s, LANES), 0)
     group = 4
 
     @pl.loop(0, cap // group)
@@ -266,7 +302,7 @@
             r = g * group + j
             row = pl.ds(r, 1)
             s_hit = jnp.where(s_iota == slot_s[row, :], 1.0, 0.0).astype(bf16)
-            pick_s[:, pl.ds(pl.multiple_of(r * LANES, LANES), LANES)] = s_hit
+            pick[:, pl.ds(pl.multiple_of(r * LANES, LANES), LANES)] = s_hit
             x_hit = x_iota == slot_x[row, :]
             upper, lower = [], []
             for k in range(FIELDS):
@@ -279,7 +315,10 @@
         acc[...] += nt(jnp.concatenate(lhs, axis=1), jnp.concatenate(rhs, axis=1))
 
     for k in range(FIELDS):
-        ext_f[k, lo:hi, :] = acc[k * cells_x : (k + 1) * cells_x, :]
+        for odd in range(2):
+            ext_f[k, pl.ds(lo + odd, half, stride=2), :] = acc[
+                k * half : (k + 1) * half, odd * cells_s : (odd + 1) * cells_s
+            ]
 
     f_x = across_blade(ext_f, lo, hi, ext_f, 12)
     for copy in f_x:
@@ -290,68 +329,84 @@
     lane = iota((8, LANES), 1)
     inside_x = ((lane >= lo) | (ib > 0)) & ((lane < hi) | (ib < n_blade - 1))
 
-    @pl.loop(0, rows)
-    def _(s):
-        inside = inside_x & (((s >= lo) | (js > 0)) & ((s < lo + cells_s) | (js < n_span - 1)))
-        at = pl.ds(pl.multiple_of(s * 8, 8), 8)
-        kappa[at, :] = jnp.where(inside, kappa[at, :], 1e-15)
+    def tile(s):
+        return pl.ds(pl.multiple_of((s + PAD) * 8, 8), 8)
+
+    def sides(s, to, count=CHUNK):
+        for j in range(count):
+            at = tile(s + j)
+            t = to[0][at, :]
+            to[1][at, :] = pltpu.roll(t, LANES - 1, 1)
+            to[2][at, :] = pltpu.roll(t, 1, 1)
+
+    @pl.loop(0, rows // 8)
+    def _(i):
+        inside = inside_x & (
+            ((i >= lo // 8) | (js > 0)) & ((i < (lo + cells_s) // 8) | (js < n_span - 1))
+        )
+        for j in range(8):
+            at = tile(i * 8 + j)
+            held = jnp.where(inside, rho[at, :], 1e15)
+            rho[at, :] = held
+            rho_up[at, :] = pltpu.roll(held, LANES - 1, 1)
+            rho_down[at, :] = pltpu.roll(held, 1, 1)
+        sides(i * 8, state_a, 8)
 
     for copy in f_x:
         copy.wait()
     for k in range(FIELDS):
         fields[k, lo : lo + cells_s, :] = ext_f[k].T
-    f_s = across_span(fields, 1, 14)
+    f_s = across_span(fields, 1, 0, 14)
     for copy in f_s:
         copy.start()
     for copy in f_s:
         copy.wait()
 
-    every = pl.ds(0, rows, stride=8)
+    every = pl.ds(PAD * 8, rows, stride=8)
     denom_add[every, :] = fields[0]
-    denom_add[pl.ds(layers - 1, rows, stride=8), :] = 0.5 * cool[...]
+    denom_add[pl.ds(PAD * 8 + layers - 1, rows, stride=8), :] = 0.5 * cool[...]
     not_last = jnp.where(iota((8, LANES), 0) < layers - 1, 1.0, 0.0)
-
-    def conduct(t, k):
-        return k + k * (t * t)
-
-    def weight(a, b):
-        return a * b / (a + b)
 
     def sweep(src, dst, step):
         first = step + 1
 
-        def tile(ref, s):
-            return ref[pl.ds(pl.multiple_of(s * 8, 8), 8), :]
-
         def chunk(i, carry):
-            t_prev, t_here, c_here, w_prev = carry
+            t_prev, t_here, r_here, w_prev = carry
+            start = first + i * CHUNK
+            sides(start - CHUNK, dst)
             for j in range(CHUNK):
-                s = first + i * CHUNK + j
-                t_next = tile(src, s + 1)
-                c_next = conduct(t_next, tile(kappa, s + 1))
-                w_next = weight(c_here, c_next)
-                w_up = weight(c_here, pltpu.roll(c_here, LANES - 1, 1))
-                w_down = pltpu.roll(w_up, 1, 1)
-                w_in = weight(c_here, pltpu.roll(c_here, 7, 0)) * not_last
+                at, after = tile(start + j), tile(start + j + 1)
+                t_next = src[0][after, :]
+                r_next = resist(t_next, rho[after, :])
+                t_up, t_down = src[1][at, :], src[2][at, :]
+                w_next = 1.0 / (r_here + r_next)
+                w_up = 1.0 / (r_here + resist(t_up, rho_up[at, :]))
+                w_down = 1.0 / (r_here + resist(t_down, rho_down[at, :]))
+                w_in = not_last / (r_here + pltpu.roll(r_here, 7, 0))
                 w_out = pltpu.roll(w_in, 1, 0)
                 numer = (
                     (w_next * t_next + w_prev * t_prev)
-                    + (w_up * pltpu.roll(t_here, LANES - 1, 1) + w_down * pltpu.roll(t_here, 1, 1))
+                    + (w_up * t_up + w_down * t_down)
                     + (w_in * pltpu.roll(t_here, 7, 0) + w_out * pltpu.roll(t_here, 1, 0))
-                    + tile(numer_add, s)
+                    + numer_add[at, :]
                 )
                 denom = ((w_next + w_prev) + (w_up + w_down)) + (
-                    (w_in + w_out) + tile(denom_add, s)
+                    (w_in + w_out) + denom_add[at, :]
                 )
-                dst[pl.ds(pl.multiple_of(s * 8, 8), 8), :] = numer / denom
-                t_prev, t_here, c_here, w_prev = t_here, t_next, c_next, w_next
-            return t_prev, t_here, c_here, w_prev
-
-        t_prev, t_here = tile(src, first - 1), tile(src, first)
-        c_prev = conduct(t_prev, tile(kappa, first - 1))
-        c_here = conduct(t_here, tile(kappa, first))
+                dst[0][at, :] = numer / denom
+                t_prev, t_here, r_here, w_prev = t_here, t_next, r_next, w_next
+            return t_prev, t_here, r_here, w_prev
+
+        def resist(t, held):
+            return held / (1.0 + t * t)
+
+        before, here = tile(first - 1), tile(first)
+        t_prev, t_here = src[0][before, :], src[0][here, :]
+        r_here = resist(t_here, rho[here, :])
+        w_prev = 1.0 / (resist(t_prev, rho[before, :]) + r_here)
         count = (rows - 2 * first + CHUNK - 1) // CHUNK
-        lax.fori_loop(0, count, chunk, (t_prev, t_here, c_here, weight(c_prev, c_here)))
+        lax.fori_loop(0, count, chunk, (t_prev, t_here, r_here, w_prev))
+        sides(first + (count - 1) * CHUNK, dst)
 
     for n in range(SUBITERS):
         extra = fields[1 + n]
@@ -362,28 +417,34 @@
         @pl.loop(0, SWEEPS // 2)
         def _(p):
             step = n * SWEEPS + 2 * p
-            sweep(temp_a, temp_b, step)
-            sweep(temp_b, temp_a, step + 1)
+            sweep(state_a, state_b, step)
+            sweep(state_b, state_a, step + 1)
 
         now = temp_a[every, :]
         tw[n] = now
-        rows_x = now[lo : lo + cells_s, :].T[lo:hi, :]
-        up, low = split(rows_x, 2)
-        wall[2 * n * cells_x : (2 * n + 1) * cells_x, :] = up
-        wall[(2 * n + 1) * cells_x : (2 * n + 2) * cells_x, :] = low
-
-    @pl.loop(0, cap)
-    def _(r):
-        row = pl.ds(r, 1)
-        lanes = pl.ds(pl.multiple_of(r * LANES, LANES), LANES)
-        found = nn(wall[...], pick_s[:, lanes])
-        x_hit = x_iota == slot_x[row, :]
-        for n in range(SUBITERS):
-            both = (
-                found[2 * n * cells_x : (2 * n + 1) * cells_x]
-                + found[(2 * n + 1) * cells_x : (2 * n + 2) * cells_x]
-            )
-            slot_v[n, row, :] = jnp.sum(jnp.where(x_hit, both, 0.0), axis=0, keepdims=True)
+        wall_x = now[lo : lo + cells_s, :].T
+        ext_c[...] = wall_x
+        for odd in range(2):
+            pieces = split(ext_c[pl.ds(lo + odd, half, stride=2), :], PIECES)
+            for p, piece in enumerate(pieces):
+                at = (n * PIECES + p) * half
+                wall[at : at + half, odd * cells_s : (odd + 1) * cells_s] = piece
+
+    @pl.loop(0, cap // 2)
+    def _(g):
+        lanes = pl.ds(pl.multiple_of(g * 2 * LANES, 2 * LANES), 2 * LANES)
+        found = nn(wall[...], pick[:, lanes])
+        for j in range(2):
+            row = pl.ds(g * 2 + j, 1)
+            x_hit = x_iota == slot_x[row, :]
+            for n in range(SUBITERS):
+                at = n * PIECES * half
+                total = found[at : at + half, j * LANES : (j + 1) * LANES]
+                for p in range(1, PIECES):
+                    total = total + found[
+                        at + p * half : at + (p + 1) * half, j * LANES : (j + 1) * LANES
+                    ]
+                slot_v[n, row, :] = jnp.sum(jnp.where(x_hit, total, 0.0), axis=0, keepdims=True)
 
     got = recv_fwd[...].reshape(LANES, LANES).T
     h = got[0:cap]
@@ -397,7 +458,7 @@
     exchange(send_back, recv_back, 1)
 
     for l in range(layers):
-        final = temp_a[pl.ds(lo * 8 + l, cells_s, stride=8), :]
+        final = temp_a[pl.ds((PAD + lo) * 8 + l, cells_s, stride=8), :]
         solid_out[l] = 2.0 * final.T[lo:hi, :]
 
     arrived(send_back, recv_back, 1)
@@ -411,7 +472,7 @@
         t_row = jnp.sum(jnp.where(at_slot, seen[cap : 2 * cap], 0.0), axis=0, keepdims=True)
         on = live[b : b + 1, :]
         flux_out[b : b + 1, :] = jnp.where(on, q_row, 0.0)
-        fluid_out[b : b + 1, :] = jnp.where(on, t_row, fluid_ref[b : b + 1, :])
+        fluid_out[b : b + 1, :] = jnp.where(on, t_row, fluid[b : b + 1, :])
 
 
 def shards(
@@ -431,10 +492,12 @@
     cap = 32
     blocks = slots // LANES
     rows = cells_s + 2 * HALO
-    tall = rows + CHUNK
+    tall = rows + 2 * PAD
     vmem = pl.BlockSpec(memory_space=pltpu.VMEM)
-    hbm = pl.BlockSpec(memory_space=pl.ANY)
+    hbm = pl.BlockSpec(memory_space=pltpu.HBM)
     big = pltpu.VMEM((tall * 8, LANES), f32)
+    faces_f = pltpu.VMEM((blocks, LANES), f32)
+    faces_i = pltpu.VMEM((blocks, LANES), jnp.int32)
     faces = pltpu.VMEM((LANES, 1, LANES), f32)
     ext = pltpu.VMEM((layers, LANES, cells_s), f32)
     temp, fluid, flux = pl.pallas_call(
@@ -444,14 +507,20 @@
             jax.ShapeDtypeStruct((blocks, LANES), f32),
             jax.ShapeDtypeStruct((blocks, LANES), f32),
         ),
-        in_specs=[hbm, hbm, vmem, vmem, vmem, vmem, vmem, vmem],
+        in_specs=[hbm] * 7 + [vmem],
         out_specs=(vmem, vmem, vmem),
         scratch_shapes=[
+            faces_f,
+            faces_f,
+            faces_i,
+            faces_i,
             ext,
             ext,
             pltpu.VMEM((LANES, cells_s), f32),
             ext,
-            pltpu.VMEM((FIELDS * cells_x, cells_s), f32),
+            pltpu.VMEM((FIELDS * cells_x // 2, 2 * cells_s), f32),
+            [big] * 3,
+            [big] * 3,
             big,
             big,
             big,
@@ -469,9 +538,9 @@
             pltpu.VMEM((cap, LANES), jnp.int32),
             pltpu.VMEM((cap, LANES), jnp.int32),
             pltpu.VMEM((FIELDS, cap, LANES), f32),
-            pltpu.VMEM((cells_s, cap * LANES), bf16),
-            pltpu.VMEM((2 * SUBITERS * cells_x, cells_s), bf16),
-            pltpu.SemaphoreType.DMA((2,)),
+            pltpu.VMEM((2 * cells_s, cap * LANES), bf16),
+            pltpu.VMEM((SUBITERS * PIECES * cells_x // 2, 2 * cells_s), bf16),
+            pltpu.SemaphoreType.DMA((7,)),
             pltpu.SemaphoreType.DMA((16,)),
             pltpu.SemaphoreType.DMA((16,)),
             pltpu.SemaphoreType.DMA((2,)),

time: 130 us -> 82.3 us (0.63)
  Pallas kernels: 122 us -> 73.9 us
    pallas_call x1, Pallas kernels: 122 us -> 73.9 us  [shards(): pl.pallas_call(functools.partial(kernel, n_blade, n_span, cap), out_shape...]
where the time goes in v2:
time: 82.3 us; the launch traced here: 81.9 us
  Pallas kernels  73.9 us (90%)
  local copies, waits for them, and re-layouts  6.68 us (8%)
  between operations  1.32 us (2%)
    pallas_call x1, Pallas kernels, shards(): pl.pallas_call(functools.partial(kernel, n_blade, n_span, cap), out_shape...  73.9 us
    unnamed x17, local copies, waits for them, and re-layouts  6.68 us

profile of v2, /device:TPU:1, one launch (start us, length us, event | category | flops | bytes accessed | tf_op | source)
XLA Modules:
  0.0 81.9 jit_solution(5970513147936999629)
XLA Ops:
  0.6 0.0 copy-start.3
  1.3 0.0 copy-done.3
  1.3 0.0 copy-start
  1.3 0.9 %copy-done = f32[8,64,128]{2,1,0:T(8,128)S(1)} copy-done((f32[8,64,128]{2,1,0:T(8,128)S(1)}, f32[8,64,128]{2,1,0:T(8,128)}, u32[]{:S(2)}) %copy-start) | copy-done | bytes 262168
  2.3 0.0 copy-start.1
  2.3 0.9 %copy-done.1 = f32[8,64,128]{2,1,0:T(8,128)S(1)} copy-done((f32[8,64,128]{2,1,0:T(8,128)S(1)}, f32[8,64,128]{2,1,0:T(8,128)}, u32[]{:S(2)}) %copy-start.1) | copy-done | bytes 262168
  3.2 0.0 copy-start.2
  3.2 0.8 copy-done.2
  4.0 0.0 copy-start.4
  4.0 0.7 copy-done.4
  4.7 0.0 copy-start.5
  4.7 0.7 copy-done.5
  5.4 0.0 copy-start.6
  5.4 0.7 copy-done.6
  6.1 73.9 %shard_map.103 = (f32[8,64,128]{2,1,0:T(8,128)S(1)}, f32[16,128]{1,0:T(8,128)S(1)}, f32[16,128]{1,0:T(8,128)S(1)}) custom-call(f32[8,64,128]{2,1,0:T(8,128)S(1)} %copy-done, f32[8,64,128]{2,1,0:T(8,128)S(1)} %copy-done.1, f32[64,128]{1,0:T(8,128)S(1)} %copy-done.2, f32[16,128]{1,0:T(8,128)S(1)} %bitcast.8, f32[16,128]{1,0:T(8,128)S(1)} %bitcast.9, ...), custom_call_target="tpu_custom_call" | custom-call | tf_op jit(solution)/shard_map/pallas_call | solution.py:503
  80.0 0.7 copy.15
  80.7 0.6 copy.16
  81.3 0.6 copy.17
Async XLA Ops:
  0.6 0.7 copy-start.3
  1.3 0.9 %copy-start = (f32[8,64,128]{2,1,0:T(8,128)S(1)}, f32[8,64,128]{2,1,0:T(8,128)}, u32[]{:S(2)}) copy-start(f32[8,64,128]{2,1,0:T(8,128)} %solid_ref.1) | copy-start | bytes 786436
  2.3 0.9 %copy-start.1 = (f32[8,64,128]{2,1,0:T(8,128)S(1)}, f32[8,64,128]{2,1,0:T(8,128)}, u32[]{:S(2)}) copy-start(f32[8,64,128]{2,1,0:T(8,128)} %kappa_ref.1) | copy-start | bytes 786436
  3.2 0.8 copy-start.2
  4.0 0.7 copy-start.4
  4.7 0.7 copy-start.5
  5.4 0.7 copy-start.6

commit v3 on v2

--- a/solution.py
+++ b/solution.py
@@ -15,6 +15,8 @@
 PIECES = 3
 CHUNK = 16
 PAD = 16
+SPAN_HALO = HALO // 2
+EDGE = 16
 MESH = pl.DeviceIdType.MESH
 f32 = jnp.float32
 bf16 = jnp.bfloat16
@@ -91,6 +93,8 @@
     halo_recv,
     face_send,
     face_recv,
+    landing,
+    landing_tw,
 ):
     devices = n_blade * n_span
     layers, cells_x, cells_s = solid_ref.shape
@@ -99,7 +103,8 @@
     ib, js = lax.axis_index("blade"), lax.axis_index("span")
     me = ib * n_span + js
     lo, hi = HALO, HALO + cells_x
-    rows = cells_s + 2 * HALO
+    s_lo, s_hi = EDGE, EDGE + cells_s
+    rows = cells_s + 2 * EDGE
 
     barrier = pltpu.get_barrier_semaphore()
 
@@ -242,29 +247,30 @@
     for copy in x_halos:
         copy.wait()
     for l in range(layers):
-        column = pl.ds((PAD + lo) * 8 + l, cells_s, stride=8)
+        column = pl.ds((PAD + s_lo) * 8 + l, cells_s, stride=8)
         temp_a[column, :] = 0.5 * ext_t[l].T
         rho[column, :] = 1.0 / ext_k[l].T
-    cool[lo : lo + cells_s, :] = ext_c[...].T
-
-    def across_span(ref, unit, pad, sem):
-        first, last = (pad + lo) * unit, (pad + lo + cells_s) * unit
-        width = HALO * unit
+    cool[s_lo:s_hi, :] = ext_c[...].T
+
+    def across_span(ref, unit, pad, count, sem, land=None):
+        first, last = (pad + s_lo) * unit, (pad + s_hi) * unit
+        width = count * unit
 
         def part(start):
             if len(ref.shape) == 3:
                 return ref.at[:, start : start + width, :]
             return ref.at[start : start + width, :]
 
+        above, below = (part(last), part(first - width)) if land is None else land
         return (
-            remote(part(first), part(last), sem, south),
-            remote(part(last - width), part(pad * unit), sem + 1, north),
+            remote(part(first), above, sem, south),
+            remote(part(last - width), below, sem + 1, north),
         )
 
     s_halos = (
-        across_span(temp_a, 8, PAD, 6)
-        + across_span(rho, 8, PAD, 8)
-        + across_span(cool, 1, 0, 10)
+        across_span(temp_a, 8, PAD, SPAN_HALO, 6)
+        + across_span(rho, 8, PAD, SPAN_HALO, 8)
+        + across_span(cool, 1, 0, EDGE, 10)
     )
     for copy in s_halos:
         copy.start()
@@ -295,37 +301,59 @@
     s_iota = iota((2 * cells_s, LANES), 0)
     group = 4
 
-    @pl.loop(0, cap // group)
-    def _(g):
-        lhs, rhs = [], []
-        for j in range(group):
-            r = g * group + j
-            row = pl.ds(r, 1)
-            s_hit = jnp.where(s_iota == slot_s[row, :], 1.0, 0.0).astype(bf16)
-            pick[:, pl.ds(pl.multiple_of(r * LANES, LANES), LANES)] = s_hit
-            x_hit = x_iota == slot_x[row, :]
-            upper, lower = [], []
-            for k in range(FIELDS):
-                v = slot_v[k, row, :]
-                v_up = v.astype(bf16).astype(f32)
-                upper.append(jnp.where(x_hit, v_up, 0.0).astype(bf16))
-                lower.append(jnp.where(x_hit, v - v_up, 0.0).astype(bf16))
-            lhs += [jnp.concatenate(upper, axis=0), jnp.concatenate(lower, axis=0)]
-            rhs += [s_hit, s_hit]
-        acc[...] += nt(jnp.concatenate(lhs, axis=1), jnp.concatenate(rhs, axis=1))
-
-    for k in range(FIELDS):
-        for odd in range(2):
-            ext_f[k, pl.ds(lo + odd, half, stride=2), :] = acc[
-                k * half : (k + 1) * half, odd * cells_s : (odd + 1) * cells_s
-            ]
-
-    f_x = across_blade(ext_f, lo, hi, ext_f, 12)
+    def scatter(fresh, chosen):
+        span = 2 * len(chosen) * half
+        base = 2 * chosen[0] * half
+
+        @pl.loop(0, cap // group)
+        def _(g):
+            lhs, rhs = [], []
+            for j in range(group):
+                r = g * group + j
+                row = pl.ds(r, 1)
+                lanes = pl.ds(pl.multiple_of(r * LANES, LANES), LANES)
+                if fresh:
+                    s_hit = jnp.where(s_iota == slot_s[row, :], 1.0, 0.0).astype(bf16)
+                    pick[:, lanes] = s_hit
+                else:
+                    s_hit = pick[:, lanes]
+                x_hit = x_iota == slot_x[row, :]
+                upper, lower = [], []
+                for k in chosen:
+                    v = slot_v[k, row, :]
+                    v_up = v.astype(bf16).astype(f32)
+                    upper.append(jnp.where(x_hit, v_up, 0.0).astype(bf16))
+                    lower.append(jnp.where(x_hit, v - v_up, 0.0).astype(bf16))
+                lhs.append(jnp.concatenate(upper + lower, axis=0))
+                rhs.append(s_hit)
+            acc[base : base + span, :] += nt(
+                jnp.concatenate(lhs, axis=1), jnp.concatenate(rhs, axis=1)
+            )
+
+        for i, k in enumerate(chosen):
+            for odd in range(2):
+                lanes = slice(odd * cells_s, (odd + 1) * cells_s)
+                up = base + i * half
+                low = up + len(chosen) * half
+                ext_f[k, pl.ds(lo + odd, half, stride=2), :] = (
+                    acc[up : up + half, lanes] + acc[low : low + half, lanes]
+                )
+
+    def turn(chosen):
+        for k in chosen:
+            fields[k, s_lo:s_hi, :] = ext_f[k].T
+
+    soon, later = range(0, 2), range(2, FIELDS)
+    ext_soon, ext_later = ext_f.at[0:2], ext_f.at[2:FIELDS]
+    scatter(True, soon)
+    f_x = across_blade(ext_soon, lo, hi, ext_soon, 12)
     for copy in f_x:
         copy.start()
-
-    for copy in s_halos:
-        copy.wait()
+    scatter(False, later)
+    late_x = across_blade(ext_later, lo, hi, ext_later, 18)
+    for copy in late_x:
+        copy.start()
+
     lane = iota((8, LANES), 1)
     inside_x = ((lane >= lo) | (ib > 0)) & ((lane < hi) | (ib < n_blade - 1))
 
@@ -339,10 +367,9 @@
             to[1][at, :] = pltpu.roll(t, LANES - 1, 1)
             to[2][at, :] = pltpu.roll(t, 1, 1)
 
-    @pl.loop(0, rows // 8)
-    def _(i):
+    def fill(i):
         inside = inside_x & (
-            ((i >= lo // 8) | (js > 0)) & ((i < (lo + cells_s) // 8) | (js < n_span - 1))
+            ((i >= s_lo // 8) | (js > 0)) & ((i < s_hi // 8) | (js < n_span - 1))
         )
         for j in range(8):
             at = tile(i * 8 + j)
@@ -352,12 +379,31 @@
             rho_down[at, :] = pltpu.roll(held, 1, 1)
         sides(i * 8, state_a, 8)
 
+    edge = EDGE // 8
+
+    @pl.loop(2 * edge, rows // 8 - 2 * edge)
+    def _(i):
+        fill(i)
+
     for copy in f_x:
         copy.wait()
-    for k in range(FIELDS):
-        fields[k, lo : lo + cells_s, :] = ext_f[k].T
-    f_s = across_span(fields, 1, 0, 14)
+    turn(soon)
+    f_s = across_span(fields.at[0:2], 1, 0, EDGE, 14)
     for copy in f_s:
+        copy.start()
+    for copy in s_halos:
+        copy.wait()
+
+    @pl.loop(0, 2 * edge)
+    def _(i):
+        fill(i)
+        fill(i + rows // 8 - 2 * edge)
+
+    for copy in late_x:
+        copy.wait()
+    turn(later)
+    late_s = across_span(fields.at[2:FIELDS], 1, 0, EDGE, 20)
+    for copy in late_s:
         copy.start()
     for copy in f_s:
         copy.wait()
@@ -368,7 +414,7 @@
     not_last = jnp.where(iota((8, LANES), 0) < layers - 1, 1.0, 0.0)
 
     def sweep(src, dst, step):
-        first = step + 1
+        first = EDGE - SPAN_HALO + 1 + step
 
         def chunk(i, carry):
             t_prev, t_here, r_here, w_prev = carry
@@ -408,7 +454,32 @@
         lax.fori_loop(0, count, chunk, (t_prev, t_here, r_here, w_prev))
         sides(first + (count - 1) * CHUNK, dst)
 
+    def find(early):
+        pair = 2 * PIECES * half
+
+        @pl.loop(0, cap // group)
+        def _(g):
+            width = group * LANES
+            lanes = pl.ds(pl.multiple_of(g * width, width), width)
+            found = nn(wall[early * PIECES * half : early * PIECES * half + pair, :], pick[:, lanes])
+            for j in range(group):
+                row = pl.ds(g * group + j, 1)
+                x_hit = x_iota == slot_x[row, :]
+                for n in range(2):
+                    at = n * PIECES * half
+                    total = found[at : at + half, j * LANES : (j + 1) * LANES]
+                    for p in range(1, PIECES):
+                        total = total + found[
+                            at + p * half : at + (p + 1) * half, j * LANES : (j + 1) * LANES
+                        ]
+                    slot_v[early + n, row, :] = jnp.sum(
+                        jnp.where(x_hit, total, 0.0), axis=0, keepdims=True
+                    )
+
     for n in range(SUBITERS):
+        if n == 1:
+            for copy in late_s:
+                copy.wait()
         extra = fields[1 + n]
         for m in range(n):
             extra = extra + tw[m] * fields[SUBITERS + n - m]
@@ -416,35 +487,36 @@
 
         @pl.loop(0, SWEEPS // 2)
         def _(p):
-            step = n * SWEEPS + 2 * p
+            step = n % 2 * SWEEPS + 2 * p
             sweep(state_a, state_b, step)
             sweep(state_b, state_a, step + 1)
 
         now = temp_a[every, :]
         tw[n] = now
-        wall_x = now[lo : lo + cells_s, :].T
-        ext_c[...] = wall_x
+        ext_c[...] = now[s_lo:s_hi, :].T
         for odd in range(2):
             pieces = split(ext_c[pl.ds(lo + odd, half, stride=2), :], PIECES)
             for p, piece in enumerate(pieces):
                 at = (n * PIECES + p) * half
                 wall[at : at + half, odd * cells_s : (odd + 1) * cells_s] = piece
-
-    @pl.loop(0, cap // 2)
-    def _(g):
-        lanes = pl.ds(pl.multiple_of(g * 2 * LANES, 2 * LANES), 2 * LANES)
-        found = nn(wall[...], pick[:, lanes])
-        for j in range(2):
-            row = pl.ds(g * 2 + j, 1)
-            x_hit = x_iota == slot_x[row, :]
-            for n in range(SUBITERS):
-                at = n * PIECES * half
-                total = found[at : at + half, j * LANES : (j + 1) * LANES]
-                for p in range(1, PIECES):
-                    total = total + found[
-                        at + p * half : at + (p + 1) * half, j * LANES : (j + 1) * LANES
-                    ]
-                slot_v[n, row, :] = jnp.sum(jnp.where(x_hit, total, 0.0), axis=0, keepdims=True)
+        if n == 1:
+            middle = across_span(
+                temp_a, 8, PAD, SPAN_HALO, 16, (landing.at[1], landing.at[0])
+            ) + across_span(
+                tw.at[0], 1, 0, EDGE, 22, (landing_tw.at[1], landing_tw.at[0])
+            )
+            for copy in middle:
+                copy.start()
+            find(0)
+            for copy in middle:
+                copy.wait()
+            for side, start in enumerate((s_lo - SPAN_HALO, s_hi)):
+                at = (start + PAD) * 8
+                temp_a[at : at + SPAN_HALO * 8, :] = landing[side]
+                sides(start, state_a, SPAN_HALO)
+                tw[0, side * s_hi : side * s_hi + EDGE, :] = landing_tw[side]
+            tw[1] = temp_a[every, :]
+    find(2)
 
     got = recv_fwd[...].reshape(LANES, LANES).T
     h = got[0:cap]
@@ -458,7 +530,7 @@
     exchange(send_back, recv_back, 1)
 
     for l in range(layers):
-        final = temp_a[pl.ds((PAD + lo) * 8 + l, cells_s, stride=8), :]
+        final = temp_a[pl.ds((PAD + s_lo) * 8 + l, cells_s, stride=8), :]
         solid_out[l] = 2.0 * final.T[lo:hi, :]
 
     arrived(send_back, recv_back, 1)
@@ -491,7 +563,7 @@
     slots = fluid_temp.shape[0]
     cap = 32
     blocks = slots // LANES
-    rows = cells_s + 2 * HALO
+    rows = cells_s + 2 * EDGE
     tall = rows + 2 * PAD
     vmem = pl.BlockSpec(memory_space=pltpu.VMEM)
     hbm = pl.BlockSpec(memory_space=pltpu.HBM)
@@ -518,7 +590,7 @@
             ext,
             pltpu.VMEM((LANES, cells_s), f32),
             ext,
-            pltpu.VMEM((FIELDS * cells_x // 2, 2 * cells_s), f32),
+            pltpu.VMEM((FIELDS * cells_x, 2 * cells_s), f32),
             [big] * 3,
             [big] * 3,
             big,
@@ -541,13 +613,15 @@
             pltpu.VMEM((2 * cells_s, cap * LANES), bf16),
             pltpu.VMEM((SUBITERS * PIECES * cells_x // 2, 2 * cells_s), bf16),
             pltpu.SemaphoreType.DMA((7,)),
-            pltpu.SemaphoreType.DMA((16,)),
-            pltpu.SemaphoreType.DMA((16,)),
+            pltpu.SemaphoreType.DMA((24,)),
+            pltpu.SemaphoreType.DMA((24,)),
             pltpu.SemaphoreType.DMA((2,)),
             pltpu.SemaphoreType.DMA((2,)),
+            pltpu.VMEM((2, SPAN_HALO * 8, LANES), f32),
+            pltpu.VMEM((2, EDGE, LANES), f32),
         ],
         compiler_params=pltpu.CompilerParams(
-            collective_id=0, has_side_effects=True, vmem_limit_bytes=48 << 20
+            collective_id=0, has_side_effects=True, vmem_limit_bytes=67043328
         ),
     )(
         solid_temp,

time: 82.3 us -> 75.1 us (0.913)
  local copies, waits for them, and re-layouts: 6.68 us -> 2.98 us
  Pallas kernels: 73.9 us -> 70.6 us
    unnamed x17 -> x7, local copies, waits for them, and re-layouts: 6.68 us -> 2.98 us
    pallas_call x1, Pallas kernels: 73.9 us -> 70.6 us  [shards(): pl.pallas_call(functools.partial(kernel, n_blade, n_span, cap), out_shape...]
where the time goes in v3:
time: 75.1 us; the launch traced here: 74.9 us
  Pallas kernels  70.6 us (94%)
  local copies, waits for them, and re-layouts  2.98 us (4%)
  between operations  1.3 us (2%)
    pallas_call x1, Pallas kernels, shards(): pl.pallas_call(functools.partial(kernel, n_blade, n_span, cap), out_shape...  70.6 us
    unnamed x7, local copies, waits for them, and re-layouts  2.98 us

profile of v3, /device:TPU:1, one launch (start us, length us, event | category | flops | bytes accessed | tf_op | source)
XLA Modules:
  0.0 74.9 jit_solution(18311717114694062834)
XLA Ops:
  1.3 70.6 %shard_map.103 = (f32[8,64,128]{2,1,0:T(8,128)}, f32[16,128]{1,0:T(8,128)}, f32[16,128]{1,0:T(8,128)}) custom-call(f32[8,64,128]{2,1,0:T(8,128)} %solid_ref.1, f32[8,64,128]{2,1,0:T(8,128)} %kappa_ref.1, f32[64,128]{1,0:T(8,128)} %cool_ref.1, f32[16,128]{1,0:T(8,128)} %bitcast.8, f32[16,128]{1,0:T(8,128)} %bitcast.9, s32[16,128]{1,0:T(8,128)} %bitcast.10, ...), custom_call_target="tpu_custom_call" | custom-call | tf_op jit(solution)/shard_map/pallas_call | solution.py:575
  71.9 0.0 copy-start.1
  71.9 1.7 %copy.15 = f32[8,64,128]{2,1,0:T(8,128)} copy(f32[8,64,128]{2,1,0:T(8,128)} %get-tuple-element.12) | data formatting | bytes 524288
  73.6 0.0 copy-done.1
  73.6 0.0 copy-start
  73.6 0.6 copy.16
  74.2 0.1 copy-done
  74.3 0.6 copy.17
Async XLA Ops:
  71.9 1.7 %copy-start.1 = (f32[16,128]{1,0:T(8,128)S(1)}, f32[16,128]{1,0:T(8,128)}, u32[]{:S(2)}) copy-start(f32[16,128]{1,0:T(8,128)} %get-tuple-element.7) | copy-start | bytes 24580
  73.6 0.7 copy-start

commit v4 on v3

--- a/solution.py
+++ b/solution.py
@@ -13,8 +13,8 @@
 LANES = 128
 FIELDS = 2 * SUBITERS
 PIECES = 3
-CHUNK = 16
-PAD = 16
+CHUNK = 24
+PAD = 24
 SPAN_HALO = HALO // 2
 EDGE = 16
 MESH = pl.DeviceIdType.MESH
@@ -531,7 +531,9 @@
 
     for l in range(layers):
         final = temp_a[pl.ds((PAD + s_lo) * 8 + l, cells_s, stride=8), :]
-        solid_out[l] = 2.0 * final.T[lo:hi, :]
+        ext_k[l, 0:cells_x, :] = 2.0 * final.T[lo:hi, :]
+    store = pltpu.make_async_copy(ext_k.at[:, 0:cells_x, :], solid_out, local_sem.at[0])
+    store.start()
 
     arrived(send_back, recv_back, 1)
     table = recv_back[...].reshape(LANES, LANES).T[0 : 2 * cap]
@@ -545,6 +547,7 @@
         on = live[b : b + 1, :]
         flux_out[b : b + 1, :] = jnp.where(on, q_row, 0.0)
         fluid_out[b : b + 1, :] = jnp.where(on, t_row, fluid[b : b + 1, :])
+    store.wait()
 
 
 def shards(
@@ -580,7 +583,7 @@
             jax.ShapeDtypeStruct((blocks, LANES), f32),
         ),
         in_specs=[hbm] * 7 + [vmem],
-        out_specs=(vmem, vmem, vmem),
+        out_specs=(hbm, vmem, vmem),
         scratch_shapes=[
             faces_f,
             faces_f,

time: 75.1 us -> 72.5 us (0.965)
  Pallas kernels: 70.6 us -> 68 us
    pallas_call x1, Pallas kernels: 70.6 us -> 68 us  [shards(): pl.pallas_call(functools.partial(kernel, n_blade, n_span, cap), out_shape...]
where the time goes in v4:
time: 72.5 us; the launch traced here: 72.3 us
  Pallas kernels  68 us (94%)
  local copies, waits for them, and re-layouts  2.98 us (4%)
  between operations  1.3 us (2%)
    pallas_call x1, Pallas kernels, shards(): pl.pallas_call(functools.partial(kernel, n_blade, n_span, cap), out_shape...  68 us
    unnamed x7, local copies, waits for them, and re-layouts  2.98 us

profile of v4, /device:TPU:1, one launch (start us, length us, event | category | flops | bytes accessed | tf_op | source)
XLA Modules:
  0.0 72.3 jit_solution(7156854710155717677)
XLA Ops:
  1.3 68.0 %shard_map.103 = (f32[8,64,128]{2,1,0:T(8,128)}, f32[16,128]{1,0:T(8,128)}, f32[16,128]{1,0:T(8,128)}) custom-call(f32[8,64,128]{2,1,0:T(8,128)} %solid_ref.1, f32[8,64,128]{2,1,0:T(8,128)} %kappa_ref.1, f32[64,128]{1,0:T(8,128)} %cool_ref.1, f32[16,128]{1,0:T(8,128)} %bitcast.8, f32[16,128]{1,0:T(8,128)} %bitcast.9, s32[16,128]{1,0:T(8,128)} %bitcast.10, ...), custom_call_target="tpu_custom_call" | custom-call | tf_op jit(solution)/shard_map/pallas_call | solution.py:578
  69.3 0.0 copy-start.1
  69.3 1.7 %copy.15 = f32[8,64,128]{2,1,0:T(8,128)} copy(f32[8,64,128]{2,1,0:T(8,128)} %get-tuple-element.12) | data formatting | bytes 524288
  71.0 0.0 copy-done.1
  71.0 0.0 copy-start
  71.0 0.6 copy.16
  71.6 0.1 copy-done
  71.7 0.6 copy.17
Async XLA Ops:
  69.3 1.7 %copy-start.1 = (f32[16,128]{1,0:T(8,128)S(1)}, f32[16,128]{1,0:T(8,128)}, u32[]{:S(2)}) copy-start(f32[16,128]{1,0:T(8,128)} %get-tuple-element.7) | copy-start | bytes 24580
  71.0 0.7 copy-start

commit v5 on v4

--- a/solution.py
+++ b/solution.py
@@ -413,13 +413,20 @@
     denom_add[pl.ds(PAD * 8 + layers - 1, rows, stride=8), :] = 0.5 * cool[...]
     not_last = jnp.where(iota((8, LANES), 0) < layers - 1, 1.0, 0.0)
 
+    def chunks(first):
+        return (rows - 2 * first + CHUNK - 1) // CHUNK
+
+    def last_chunk(first):
+        return first + (chunks(first) - 1) * CHUNK
+
     def sweep(src, dst, step):
         first = EDGE - SPAN_HALO + 1 + step
 
-        def chunk(i, carry):
+        def chunk(i, carry, done=None):
             t_prev, t_here, r_here, w_prev = carry
             start = first + i * CHUNK
-            sides(start - CHUNK, dst)
+            if done is None:
+                sides(start - CHUNK, dst)
             for j in range(CHUNK):
                 at, after = tile(start + j), tile(start + j + 1)
                 t_next = src[0][after, :]
@@ -441,6 +448,8 @@
                 )
                 dst[0][at, :] = numer / denom
                 t_prev, t_here, r_here, w_prev = t_here, t_next, r_next, w_next
+            if done is not None:
+                sides(done, src)
             return t_prev, t_here, r_here, w_prev
 
         def resist(t, held):
@@ -450,20 +459,19 @@
         t_prev, t_here = src[0][before, :], src[0][here, :]
         r_here = resist(t_here, rho[here, :])
         w_prev = 1.0 / (resist(t_prev, rho[before, :]) + r_here)
-        count = (rows - 2 * first + CHUNK - 1) // CHUNK
-        lax.fori_loop(0, count, chunk, (t_prev, t_here, r_here, w_prev))
-        sides(first + (count - 1) * CHUNK, dst)
+        carry = chunk(0, (t_prev, t_here, r_here, w_prev), last_chunk(first - 1))
+        lax.fori_loop(1, chunks(first), chunk, carry)
 
     def find(early):
         pair = 2 * PIECES * half
 
-        @pl.loop(0, cap // group)
+        @pl.loop(0, cap // 8)
         def _(g):
-            width = group * LANES
+            width = 8 * LANES
             lanes = pl.ds(pl.multiple_of(g * width, width), width)
             found = nn(wall[early * PIECES * half : early * PIECES * half + pair, :], pick[:, lanes])
-            for j in range(group):
-                row = pl.ds(g * group + j, 1)
+            for j in range(8):
+                row = pl.ds(g * 8 + j, 1)
                 x_hit = x_iota == slot_x[row, :]
                 for n in range(2):
                     at = n * PIECES * half
@@ -508,6 +516,7 @@
             for copy in middle:
                 copy.start()
             find(0)
+            sides(last_chunk(s_lo), state_a)
             for copy in middle:
                 copy.wait()
             for side, start in enumerate((s_lo - SPAN_HALO, s_hi)):

time: 72.5 us -> 69.1 us (0.953)
  Pallas kernels: 68 us -> 64.6 us
    pallas_call x1, Pallas kernels: 68 us -> 64.6 us  [shards(): pl.pallas_call(functools.partial(kernel, n_blade, n_span, cap), out_shape...]
where the time goes in v5:
time: 69.1 us; the launch traced here: 68.9 us
  Pallas kernels  64.6 us (93%)
  local copies, waits for them, and re-layouts  2.98 us (4%)
  between operations  1.3 us (2%)
    pallas_call x1, Pallas kernels, shards(): pl.pallas_call(functools.partial(kernel, n_blade, n_span, cap), out_shape...  64.6 us
    unnamed x7, local copies, waits for them, and re-layouts  2.98 us

profile of v5, /device:TPU:1, one launch (start us, length us, event | category | flops | bytes accessed | tf_op | source)
XLA Modules:
  0.0 68.9 jit_solution(8993970206716649282)
XLA Ops:
  1.3 64.6 %shard_map.103 = (f32[8,64,128]{2,1,0:T(8,128)}, f32[16,128]{1,0:T(8,128)}, f32[16,128]{1,0:T(8,128)}) custom-call(f32[8,64,128]{2,1,0:T(8,128)} %solid_ref.1, f32[8,64,128]{2,1,0:T(8,128)} %kappa_ref.1, f32[64,128]{1,0:T(8,128)} %cool_ref.1, f32[16,128]{1,0:T(8,128)} %bitcast.8, f32[16,128]{1,0:T(8,128)} %bitcast.9, s32[16,128]{1,0:T(8,128)} %bitcast.10, ...), custom_call_target="tpu_custom_call" | custom-call | tf_op jit(solution)/shard_map/pallas_call | solution.py:587
  65.9 0.0 copy-start.1
  65.9 1.7 %copy.15 = f32[8,64,128]{2,1,0:T(8,128)} copy(f32[8,64,128]{2,1,0:T(8,128)} %get-tuple-element.12) | data formatting | bytes 524288
  67.6 0.0 copy-done.1
  67.6 0.0 copy-start
  67.6 0.6 copy.16
  68.2 0.1 copy-done
  68.3 0.6 copy.17
Async XLA Ops:
  65.9 1.7 %copy-start.1 = (f32[16,128]{1,0:T(8,128)S(1)}, f32[16,128]{1,0:T(8,128)}, u32[]{:S(2)}) copy-start(f32[16,128]{1,0:T(8,128)} %get-tuple-element.7) | copy-start | bytes 24580
  67.6 0.7 %copy-start = (f32[16,128]{1,0:T(8,128)S(1)}, f32[16,128]{1,0:T(8,128)}, u32[]{:S(2)}) copy-start(f32[16,128]{1,0:T(8,128)} %get-tuple-element.8) | copy-start | bytes 24580

commit v6 on v5

--- a/solution.py
+++ b/solution.py
@@ -299,7 +299,7 @@
     half = cells_x // 2
     x_iota = iota((half, LANES), 0)
     s_iota = iota((2 * cells_s, LANES), 0)
-    group = 4
+    group = 8
 
     def scatter(fresh, chosen):
         span = 2 * len(chosen) * half

time: 69.1 us -> 68 us (0.984)
  Pallas kernels: 64.6 us -> 63.6 us
    pallas_call x1, Pallas kernels: 64.6 us -> 63.6 us  [shards(): pl.pallas_call(functools.partial(kernel, n_blade, n_span, cap), out_shape...]
where the time goes in v6:
time: 68 us; the launch traced here: 67.9 us
  Pallas kernels  63.6 us (94%)
  local copies, waits for them, and re-layouts  2.98 us (4%)
  between operations  1.3 us (2%)
    pallas_call x1, Pallas kernels, shards(): pl.pallas_call(functools.partial(kernel, n_blade, n_span, cap), out_shape...  63.6 us
    unnamed x7, local copies, waits for them, and re-layouts  2.98 us

profile of v6, /device:TPU:1, one launch (start us, length us, event | category | flops | bytes accessed | tf_op | source)
XLA Modules:
  0.0 67.9 jit_solution(14935325089422751024)
XLA Ops:
  1.3 63.6 %shard_map.103 = (f32[8,64,128]{2,1,0:T(8,128)}, f32[16,128]{1,0:T(8,128)}, f32[16,128]{1,0:T(8,128)}) custom-call(f32[8,64,128]{2,1,0:T(8,128)} %solid_ref.1, f32[8,64,128]{2,1,0:T(8,128)} %kappa_ref.1, f32[64,128]{1,0:T(8,128)} %cool_ref.1, f32[16,128]{1,0:T(8,128)} %bitcast.8, f32[16,128]{1,0:T(8,128)} %bitcast.9, s32[16,128]{1,0:T(8,128)} %bitcast.10, ...), custom_call_target="tpu_custom_call" | custom-call | tf_op jit(solution)/shard_map/pallas_call | solution.py:587
  64.9 0.0 copy-start.1
  64.9 1.7 %copy.15 = f32[8,64,128]{2,1,0:T(8,128)} copy(f32[8,64,128]{2,1,0:T(8,128)} %get-tuple-element.12) | data formatting | bytes 524288
  66.5 0.0 copy-done.1
  66.5 0.0 copy-start
  66.6 0.6 copy.16
  67.2 0.1 copy-done
  67.3 0.6 copy.17
Async XLA Ops:
  64.9 1.7 %copy-start.1 = (f32[16,128]{1,0:T(8,128)S(1)}, f32[16,128]{1,0:T(8,128)}, u32[]{:S(2)}) copy-start(f32[16,128]{1,0:T(8,128)} %get-tuple-element.7) | copy-start | bytes 24580
  66.5 0.7 %copy-start = (f32[16,128]{1,0:T(8,128)S(1)}, f32[16,128]{1,0:T(8,128)}, u32[]{:S(2)}) copy-start(f32[16,128]{1,0:T(8,128)} %get-tuple-element.8) | copy-start | bytes 24580
